TPU v7x, 32 devices: a whole 2x2x4 slice. The times are simulated.
32 devices in a mesh: rcv: 16 (over z, x, core), frq: 2 (over y).
Axes of the slice: x: 2, y: 2, z: 4, core: 2. Of those that a mesh axis runs over, the one named last changes fastest.
Arguments:
- spectra: bfloat16 [2, 256, 128, 4096], P(None, None, 'frq', 'rcv'), may hold values from -6 to 6
- virtual_sources: int32 [128], replicated, may hold values from 0 to 4095, as said below
- references: int32 [256], replicated, may hold values from 0 to 4095, as said below
- coda_start: int32 [128], replicated, may hold values from 64 to 255
- coda_end: int32 [128], replicated, may hold values from 384 to 511
Outputs:
- correlations: float32 [2, 128, 256, 4096], P(None, 'frq', None, 'rcv')
Inputs may be any that keep to these rules, and one draw needn't show every extreme that they name: `virtual_sources`: distinct receivers; virtual source v is one of the receivers (v // 8) * 256 to (v // 8 + 1) * 256 - 1. `references`: distinct receivers; reference p is one of the receivers (p // 16) * 256 to (p // 16 + 1) * 256 - 1.
All inputs are finite; a program needn't handle non-finite values.
Results may differ from a plain program's by a relative error of at most 0.0068.
Values may be sent and summed in bfloat16 or wider, within the bound.
No kernel may reach another device: no remote copies, remote signals or barrier semaphores. Data moves between devices by JAX's collectives and lax.ppermute only.
A program may use at most 192 MiB of HBM per device.

v0:
```python
import math

import jax
import jax.numpy as jnp
from jax import lax
from jax.sharding import PartitionSpec as P

L = 1024


def lag_tables(freq_count, lag_count, first_lag, lag_width):
    lag_values = first_lag + jnp.arange(lag_width, dtype=jnp.int32)
    bin_numbers = jnp.arange(freq_count, dtype=jnp.int32) + 1
    phase_steps = bin_numbers[:, None] * lag_values[None, :] % lag_count
    angles = phase_steps.astype(jnp.float32) * (2.0 * math.pi / lag_count)
    return (jnp.cos(angles), jnp.sin(angles))


def taper_weights(coda_start, coda_end, lag_count):
    lag_values = jnp.arange(lag_count, dtype=jnp.int32)
    lag_reach = jnp.where(lag_values < lag_count // 2, lag_values, lag_count - lag_values)[:, None]
    coda_first = coda_start[None, :]
    coda_last = coda_end[None, :]
    inside = (lag_reach >= coda_first) & (lag_reach < coda_last)
    window_span = (coda_last - coda_first).astype(jnp.float32)
    sine_value = jnp.sin(
        math.pi * ((lag_reach - coda_first).astype(jnp.float32) + 0.5) / window_span
    )
    return jnp.where(inside, sine_value * sine_value, jnp.zeros_like(sine_value))


def recompress(spectra_block, taper_table, lag_count):
    freq_count = spectra_block.shape[1]
    src_count = spectra_block.shape[2]
    rcv_count = spectra_block.shape[3]
    flattened = spectra_block.reshape(2 * freq_count, src_count * rcv_count)
    lag_width = min(lag_count, 256)
    accumulated = jnp.zeros((2 * freq_count, src_count * rcv_count), jnp.float32)
    for lag_block in range(lag_count // lag_width):
        first_lag = lag_block * lag_width
        cosine_table, sine_table = lag_tables(freq_count, lag_count, first_lag, lag_width)
        stacked = jnp.concatenate([cosine_table, -sine_table], axis=0)
        inverse = (stacked.T * (1.0 / math.sqrt(freq_count))).astype(jnp.bfloat16)
        forward = (stacked * (4.0 / math.sqrt(lag_count))).astype(jnp.bfloat16)
        series = jnp.dot(inverse, flattened, preferred_element_type=jnp.float32)
        weights = taper_table[first_lag : first_lag + lag_width]
        shaped = series.reshape(lag_width, src_count, rcv_count) * weights[:, :, None]
        squashed = (shaped / jnp.sqrt(1.0 + shaped * shaped)).astype(jnp.bfloat16)
        squashed = squashed.reshape(lag_width, src_count * rcv_count)
        accumulated = accumulated + jnp.dot(forward, squashed, preferred_element_type=jnp.float32)
    return accumulated.astype(jnp.bfloat16).reshape(2, freq_count, src_count, rcv_count)


def cross_spectra(sources, spectra_block):
    window_count = spectra_block.shape[1]
    left_side = jnp.concatenate([sources[0], sources[1]], axis=0)
    right_real = jnp.concatenate([spectra_block[0], spectra_block[1]], axis=0)
    right_imag = jnp.concatenate([spectra_block[1], -spectra_block[0]], axis=0)
    real_part = jnp.einsum(
        "wfv,wfr->fvr", left_side, right_real, preferred_element_type=jnp.float32
    )
    imag_part = jnp.einsum(
        "wfv,wfr->fvr", left_side, right_imag, preferred_element_type=jnp.float32
    )
    return (jnp.stack([real_part, imag_part]) / math.sqrt(window_count)).astype(jnp.bfloat16)


def recorrelate(picked, relayed):
    src_total = picked.shape[2]
    left_side = jnp.concatenate([picked[0], picked[1]], axis=1)
    right_real = jnp.concatenate([relayed[0], relayed[1]], axis=1)
    right_imag = jnp.concatenate([relayed[1], -relayed[0]], axis=1)
    real_part = jnp.einsum(
        "fvp,fvr->fpr", left_side, right_real, preferred_element_type=jnp.float32
    )
    imag_part = jnp.einsum(
        "fvp,fvr->fpr", left_side, right_imag, preferred_element_type=jnp.float32
    )
    return jnp.stack([real_part, imag_part]) / math.sqrt(src_total)


def body(spectra, virtual_sources, references, coda_start, coda_end):
    rcv_dev = spectra.shape[3]
    rcv_index = lax.axis_index("rcv")
    rcv_total = lax.axis_size("rcv")
    first_rcv = rcv_index * rcv_dev
    local_rows = jnp.arange(rcv_dev, dtype=jnp.int32)
    per_device = virtual_sources.shape[0] // rcv_total
    own_picks = (
        lax.dynamic_slice_in_dim(virtual_sources, rcv_index * per_device, per_device) - first_rcv
    )
    onehot = (local_rows[:, None] == own_picks[None, :]).astype(jnp.bfloat16)
    selected = jnp.einsum("cwfr,rv->cwfv", spectra, onehot, preferred_element_type=jnp.float32)
    sources = lax.all_gather(selected.astype(jnp.bfloat16), "rcv", axis=3, tiled=True)
    cross_spec = cross_spectra(sources, spectra)
    taper_table = taper_weights(coda_start, coda_end, L)
    spread = lax.all_to_all(cross_spec, "frq", split_axis=3, concat_axis=1, tiled=True)
    relaid = recompress(spread, taper_table, L)
    returned = lax.all_to_all(relaid, "frq", split_axis=1, concat_axis=3, tiled=True)
    ref_share = references.shape[0] // rcv_total
    own_refs = lax.dynamic_slice_in_dim(references, rcv_index * ref_share, ref_share) - first_rcv
    ref_onehot = (local_rows[:, None] == own_refs[None, :]).astype(jnp.bfloat16)
    ref_terms = jnp.einsum(
        "cfvr,rp->cfvp", returned, ref_onehot, preferred_element_type=jnp.float32
    )
    picked = lax.all_gather(ref_terms.astype(jnp.bfloat16), "rcv", axis=3, tiled=True)
    return recorrelate(picked, returned)


def solution(mesh):
    return jax.shard_map(
        body,
        mesh=mesh,
        in_specs=(P(None, None, "frq", "rcv"), P(), P(), P(), P()),
        out_specs=P(None, "frq", None, "rcv"),
        check_vma=False,
    )
```

profile of v0, /device:TPU:0, one launch (start us, length us, event | category | flops | bytes accessed | tf_op | source)
XLA Modules:
  0.0 694.7 jit_solution(1139606095262751912)
XLA Ops:
  6.5 0.7 dynamic-slice_subtract_fusion.1
  7.3 21.1 %fusion.23 = bf16[2,256,64,8]{1,3,2,0:T(8,128)(2,1)} fusion(s32[8]{0:T(128)S(1)} %dynamic-slice_subtract_fusion.1, bf16[2,256,64,256]{3,2,1,0:T(8,128)(2,1)} %param.5), kind=kOutput, calls=%fused_computation.42 | convolution fusion | flops 134481920 | bytes 17301536 | tf_op jit(solution)/shard_map/cwfr,rv->cwfv/dot_general | solution.py:93
  28.4 0.0 all-gather.3.cloned.1.call-update
  28.4 16.4 %copy.16 = bf16[2,256,64,256]{3,1,2,0:T(8,128)(2,1)} copy(bf16[2,256,64,256]{3,2,1,0:T(8,128)(2,1)} %param.5) | data formatting | bytes 33554432 | tf_op args[0]
  44.9 7.2 %fusion.86 = bf16[256,64,256]{2,0,1:T(8,128)(2,1)} fusion(bf16[2,256,64,256]{3,1,2,0:T(8,128)(2,1)} %copy.16), kind=kLoop, calls=%fused_computation.144 | loop fusion | flops 4194304 | bytes 16777216 | tf_op jit(solution)/shard_map/neg | solution.py:58
  52.0 11.7 %slice_bitcast_fusion.1 = (bf16[256,64,256]{2,0,1:T(8,128)(2,1)}, bf16[256,64,256]{2,0,1:T(8,128)(2,1)}) fusion(bf16[2,256,64,256]{3,1,2,0:T(8,128)(2,1)} %copy.16), kind=kLoop, calls=%fused_computation.23 | loop fusion | bytes 33554432 | tf_op jit(solution)/shard_map/squeeze | solution.py:57
  63.7 45.3 %all-gather.3.cloned.1.call-done = bf16[2,256,64,128]{1,3,2,0:T(8,128)(2,1)} async-done(((bf16[2,256,64,8]{1,3,2,0:T(8,128)(2,1)}), bf16[2,256,64,128]{1,3,2,0:T(8,128)(2,1)}) %all-gather.3.cloned.1.call-update) | async-done | bytes 8388624 | tf_op jit(solution)/shard_map/all_gather | solution.py:94
  109.0 6.0 slice_bitcast_fusion.5
  115.0 13.2 %fusion.20 = f32[1,64,128,256]{3,2,1,0:T(8,128)} fusion(bf16[256,64,256]{2,0,1:T(8,128)(2,1)} %get-tuple-element.6, bf16[256,64,256]{2,0,1:T(8,128)(2,1)} %get-tuple-element.5, bf16[256,64,128]{0,2,1:T(8,128)(2,1)} %get-tuple-element.12, bf16[256,64,128]{0,2,1:T(8,128)(2,1)} %get-tuple-element.11), kind=kOutput, calls=%fused_computation.39 | convolution fusion | flops 2197815296 | bytes 33554432 | tf_op jit(solution)/shard_map/wfv,wfr->fvr/dot_general | solution.py:59
  128.2 13.0 %fusion.17 = f32[1,64,128,256]{3,2,1,0:T(8,128)} fusion(bf16[256,64,256]{2,0,1:T(8,128)(2,1)} %fusion.86, bf16[256,64,256]{2,0,1:T(8,128)(2,1)} %get-tuple-element.6, bf16[256,64,128]{0,2,1:T(8,128)(2,1)} %get-tuple-element.12, bf16[256,64,128]{0,2,1:T(8,128)(2,1)} %get-tuple-element.11), kind=kOutput, calls=%fused_computation.38 | convolution fusion | flops 2197815296 | bytes 33554432 | tf_op jit(solution)/shard_map/wfv,wfr->fvr/dot_general | solution.py:62
  141.3 9.7 %fusion.9 = bf16[2,64,128,256]{3,2,1,0:T(8,128)(2,1)} fusion(f32[1,64,128,256]{3,2,1,0:T(8,128)} %fusion.17, f32[1,64,128,256]{3,2,1,0:T(8,128)} %fusion.20), kind=kLoop, calls=%fused_computation.14 | loop fusion | flops 12582912 | bytes 25165824 | tf_op jit(solution)/shard_map/convert_element_type | solution.py:65
  151.0 11.9 %copy.19 = bf16[2,64,128,256]{2,1,0,3:T(8,128)(2,1)} copy(bf16[2,64,128,256]{3,2,1,0:T(8,128)(2,1)} %fusion.9) | data formatting | bytes 16777216 | tf_op jit(solution)/shard_map/convert_element_type | solution.py:65
  162.9 7.1 %all-to-all-start = ((bf16[2,64,128,256]{2,1,0,3:T(8,128)(2,1)}), bf16[2,64,128,256]{2,1,0,3:T(8,128)(2,1)}, u32[]{:S(2)}, u32[]{:S(2)}) async-start(bf16[2,64,128,256]{2,1,0,3:T(8,128)(2,1)} %copy.19), calls=%async_computation | async-start | bytes 16777216 | tf_op jit(solution)/shard_map/all_to_all | solution.py:97
  170.0 1.9 multiply_select_fusion
  172.0 2.1 fusion.57
  174.1 88.8 %all-to-all-done = bf16[2,64,128,256]{2,1,0,3:T(8,128)(2,1)} async-done(((bf16[2,64,128,256]{2,1,0,3:T(8,128)(2,1)}), bf16[2,64,128,256]{2,1,0,3:T(8,128)(2,1)}, u32[]{:S(2)}, u32[]{:S(2)}) %all-to-all-start) | async-done | bytes 8388640 | tf_op jit(solution)/shard_map/all_to_all | solution.py:97
  263.0 12.5 %copy.20 = bf16[2,64,128,2,128]{4,2,1,3,0:T(8,128)(2,1)} copy(bf16[2,64,128,2,128]{2,1,0,4,3:T(8,128)(2,1)} %bitcast.10) | data formatting | bytes 16777216 | tf_op jit(solution)/shard_map/all_to_all | solution.py:97
  275.5 23.1 %copy.32 = bf16[32,8,128,128]{3,1,2,0:T(8,128)(2,1)} copy(bf16[32,8,128,128]{3,2,1,0:T(8,128)(2,1)} %bitcast.80) | data formatting | bytes 16777216
  298.6 11.9 %copy.21 = bf16[16384,256]{1,0:T(8,128)(2,1)} copy(bf16[16384,256]{0,1:T(8,128)(2,1)} %bitcast.81) | data formatting | bytes 16777216 | tf_op jit(solution)/shard_map/dot_general | solution.py:45
  310.5 8.1 %multiply_convert_fusion.3 = bf16[256,128,128]{0,2,1:T(8,128)(2,1)S(1)} fusion(bf16[128,128,256]{2,1,0:T(8,128)(2,1)} %bitcast.86, f32[256,128]{0,1:T(8,128)S(1)} %get-tuple-element.16, f32[128,256]{1,0:T(8,128)S(1)} %get-tuple-element.23, f32[128,256]{1,0:T(8,128)S(1)} %get-tuple-element.28), kind=kOutput, calls=%fused_computation.18 | convolution fusion | flops 2168651776 | bytes 17170432 | tf_op jit(solution)/shard_map/dot_general | solution.py:45
  318.7 8.5 %fusion.36 = f32[256,16384]{1,0:T(8,128)} fusion(bf16[256,16384]{0,1:T(8,128)(2,1)S(1)} %bitcast.85, f32[128,256]{1,0:T(8,128)S(1)} %get-tuple-element.23, f32[128,256]{1,0:T(8,128)S(1)} %get-tuple-element.28), kind=kOutput, calls=%fused_computation.86 | convolution fusion | flops 2147680256 | bytes 25427968 | tf_op jit(solution)/shard_map/dot_general | solution.py:50
  327.2 10.3 %multiply_convert_fusion.2 = bf16[256,128,128]{0,2,1:T(8,128)(2,1)} fusion(bf16[128,128,256]{2,1,0:T(8,128)(2,1)} %bitcast.87, f32[256,128]{0,1:T(8,128)S(1)} %get-tuple-element.15, f32[128,256]{1,0:T(8,128)S(1)} %get-tuple-element.24, f32[128,256]{1,0:T(8,128)S(1)} %get-tuple-element.25), kind=kOutput, calls=%fused_computation.17 | convolution fusion | flops 2168651776 | bytes 17170432 | tf_op jit(solution)/shard_map/dot_general | solution.py:45
  337.5 16.7 %convolution_add_fusion.2 = f32[256,16384]{1,0:T(8,128)} fusion(f32[256,16384]{1,0:T(8,128)} %fusion.36, bf16[256,16384]{0,1:T(8,128)(2,1)} %bitcast.83, f32[128,256]{1,0:T(8,128)S(1)} %get-tuple-element.24, f32[128,256]{1,0:T(8,128)S(1)} %get-tuple-element.25), kind=kOutput, calls=%fused_computation.3 | convolution fusion | flops 2151874560 | bytes 42205184 | tf_op jit(solution)/shard_map/dot_general | solution.py:50
  354.2 10.1 %multiply_convert_fusion.1 = bf16[256,128,128]{0,2,1:T(8,128)(2,1)} fusion(bf16[128,128,256]{2,1,0:T(8,128)(2,1)} %bitcast.88, f32[256,128]{0,1:T(8,128)S(1)} %get-tuple-element.14, f32[128,256]{1,0:T(8,128)S(1)} %get-tuple-element.26, f32[128,256]{1,0:T(8,128)S(1)} %get-tuple-element.27), kind=kOutput, calls=%fused_computation.16 | convolution fusion | flops 2168651776 | bytes 17170432 | tf_op jit(solution)/shard_map/dot_general | solution.py:45
  364.3 16.7 %convolution_add_fusion.1 = f32[256,16384]{1,0:T(8,128)} fusion(f32[256,16384]{1,0:T(8,128)} %convolution_add_fusion.2, bf16[256,16384]{0,1:T(8,128)(2,1)} %bitcast.84, f32[128,256]{1,0:T(8,128)S(1)} %get-tuple-element.26, f32[128,256]{1,0:T(8,128)S(1)} %get-tuple-element.27), kind=kOutput, calls=%fused_computation.2 | convolution fusion | flops 2151874560 | bytes 42205184 | tf_op jit(solution)/shard_map/dot_general | solution.py:50
  381.0 10.4 %multiply_convert_fusion = bf16[256,128,128]{0,2,1:T(8,128)(2,1)} fusion(bf16[128,128,256]{2,1,0:T(8,128)(2,1)} %bitcast.89, f32[256,128]{0,1:T(8,128)S(1)} %get-tuple-element.13, f32[128,256]{1,0:T(8,128)S(1)} %get-tuple-element.18, f32[128,256]{1,0:T(8,128)S(1)} %get-tuple-element.17), kind=kOutput, calls=%fused_computation.15 | convolution fusion | flops 2168651776 | bytes 17170432 | tf_op jit(solution)/shard_map/dot_general | solution.py:45
  391.4 13.5 %fusion.16 = bf16[32,8,128,128]{3,1,2,0:T(8,128)(2,1)} fusion(f32[256,16384]{1,0:T(8,128)} %convolution_add_fusion.1, bf16[256,16384]{0,1:T(8,128)(2,1)} %bitcast.90, f32[128,256]{1,0:T(8,128)S(1)} %get-tuple-element.18, f32[128,256]{1,0:T(8,128)S(1)} %get-tuple-element.17), kind=kOutput, calls=%fused_computation.33 | convolution fusion | flops 2156068864 | bytes 33816576 | tf_op jit(solution)/shard_map/dot_general | solution.py:50
  404.9 9.4 %copy.27 = bf16[32,8,128,128]{3,2,1,0:T(8,128)(2,1)} copy(bf16[32,8,128,128]{3,1,2,0:T(8,128)(2,1)} %fusion.16) | data formatting | bytes 16777216
  414.3 10.3 %copy.22 = bf16[2,128,128,128]{3,2,0,1:T(8,128)(2,1)} copy(bf16[2,128,128,128]{3,2,1,0:T(8,128)(2,1)} %bitcast.82) | data formatting | bytes 16777216 | tf_op jit(solution)/shard_map/reshape | solution.py:51
  424.6 7.1 %all-to-all-start.1 = ((bf16[2,128,128,128]{3,2,0,1:T(8,128)(2,1)}), bf16[2,128,128,128]{3,2,0,1:T(8,128)(2,1)}, u32[]{:S(2)}, u32[]{:S(2)}) async-start(bf16[2,128,128,128]{3,2,0,1:T(8,128)(2,1)} %copy.22), calls=%async_computation.1 | async-start | bytes 16777216 | tf_op jit(solution)/shard_map/all_to_all | solution.py:99
  431.7 0.0 all-gather.5.cloned.1.call-start
  431.8 0.1 dynamic-slice_subtract_fusion
  431.9 92.0 %all-to-all-done.1 = bf16[2,128,128,128]{3,2,0,1:T(8,128)(2,1)} async-done(((bf16[2,128,128,128]{3,2,0,1:T(8,128)(2,1)}), bf16[2,128,128,128]{3,2,0,1:T(8,128)(2,1)}, u32[]{:S(2)}, u32[]{:S(2)}) %all-to-all-start.1) | async-done | bytes 8388640 | tf_op jit(solution)/shard_map/all_to_all | solution.py:99
  523.9 16.7 %copy.33 = bf16[2,2,64,128,128]{4,1,3,2,0:T(2,128)(2,1)} copy(bf16[2,2,64,128,128]{4,3,0,2,1:T(8,128)(2,1)} %bitcast.21) | data formatting | bytes 16777216 | tf_op jit(solution)/shard_map/all_to_all | solution.py:99
  540.6 14.1 %all_to_all.30 = bf16[2,64,128,256]{3,2,1,0:T(8,128)(2,1)} reshape(bf16[2,64,128,2,128]{4,3,2,1,0:T(2,128)(2,1)} %bitcast.78) | data formatting | bytes 16777216 | tf_op jit(solution)/shard_map/all_to_all | solution.py:99
  554.7 6.5 convolution_convert_fusion
  561.2 0.0 all-gather.5.cloned.1.call-update
  561.2 8.7 %fusion.88 = (bf16[1,64,128,2,128]{4,3,2,1,0:T(2,128)(2,1)}, bf16[1,64,128,2,128]{4,3,2,1,0:T(2,128)(2,1)}) fusion(bf16[2,64,128,2,128]{4,3,2,1,0:T(2,128)(2,1)} %bitcast.79), kind=kLoop, calls=%fused_computation.146 | loop fusion | bytes 16777216 | tf_op jit(solution)/shard_map/slice | solution.py:71
  569.9 7.7 %squeeze.35 = bf16[64,128,256]{2,1,0:T(8,128)(2,1)} reshape(bf16[1,64,128,2,128]{4,3,2,1,0:T(2,128)(2,1)} %get-tuple-element.9) | data formatting | bytes 8388608 | tf_op jit(solution)/shard_map/squeeze | solution.py:71
  577.6 7.6 %squeeze.34 = bf16[64,128,256]{2,1,0:T(8,128)(2,1)} reshape(bf16[1,64,128,2,128]{4,3,2,1,0:T(2,128)(2,1)} %get-tuple-element.10) | data formatting | bytes 8388608 | tf_op jit(solution)/shard_map/squeeze | solution.py:71
  585.2 5.4 neg.23
  590.6 45.7 %all-gather.5.cloned.1.call-done = bf16[2,64,128,256]{2,3,1,0:T(8,128)(2,1)} async-done(((bf16[2,64,128,16]{2,3,1,0:T(8,128)(2,1)}), bf16[2,64,128,256]{2,3,1,0:T(8,128)(2,1)}) %all-gather.5.cloned.1.call-update) | async-done | bytes 8388624 | tf_op jit(solution)/shard_map/all_gather | solution.py:106
  636.3 7.0 %slice_bitcast_fusion.3 = (bf16[64,128,256]{1,2,0:T(8,128)(2,1)}, bf16[64,128,256]{1,2,0:T(8,128)(2,1)}) fusion(bf16[2,64,128,256]{2,3,1,0:T(8,128)(2,1)} %all-gather.5.cloned.1.call-done), kind=kLoop, calls=%fused_computation.35 | loop fusion | bytes 16777216 | tf_op jit(solution)/shard_map/squeeze | solution.py:70
  643.3 0.0 copy-done
  643.3 1.8 copy-done.1
  645.2 9.3 %convolution_bitcast_fusion.1 = f32[1,64,256,256]{3,2,1,0:T(8,128)} fusion(bf16[64,128,256]{2,1,0:T(8,128)(2,1)S(1)} %copy-done.1, bf16[64,128,256]{2,1,0:T(8,128)(2,1)S(1)} %copy-done, bf16[64,128,256]{1,2,0:T(8,128)(2,1)} %get-tuple-element.8, bf16[64,128,256]{1,2,0:T(8,128)(2,1)} %get-tuple-element.7), kind=kOutput, calls=%fused_computation.20 | convolution fusion | flops 2181038080 | bytes 33554432 | tf_op jit(solution)/shard_map/fvp,fvr->fpr/dot_general | solution.py:73
  654.4 9.9 %convolution_bitcast_fusion = f32[1,64,256,256]{3,2,1,0:T(8,128)} fusion(bf16[64,128,256]{2,1,0:T(8,128)(2,1)} %neg.23, bf16[64,128,256]{2,1,0:T(8,128)(2,1)S(1)} %copy-done.1, bf16[64,128,256]{1,2,0:T(8,128)(2,1)} %get-tuple-element.8, bf16[64,128,256]{1,2,0:T(8,128)(2,1)} %get-tuple-element.7), kind=kOutput, calls=%fused_computation.19 | convolution fusion | flops 2181038080 | bytes 33554432 | tf_op jit(solution)/shard_map/fvp,fvr->fpr/dot_general | solution.py:76
  664.3 23.1 %maximum_multiply_fusion = f32[2,64,256,256]{3,2,1,0:T(8,128)} fusion(f32[1,64,256,256]{3,2,1,0:T(8,128)} %convolution_bitcast_fusion, f32[1,64,256,256]{3,2,1,0:T(8,128)} %convolution_bitcast_fusion.1), kind=kLoop, calls=%fused_computation | loop fusion | flops 16777216 | bytes 67108864 | tf_op jit(solution)/shard_map/div | solution.py:79
  (15 shorter events, 0.1 us)
Async XLA Ops:
  6.5 102.5 %all-gather.3.cloned.1.call-start = ((), (), s32[]{:S(2)}) async-start(), calls=%async_computation.2 | async-start | bytes 8912896 | tf_op jit(solution)/shard_map/all_gather | solution.py:94
  162.9 7.1 %copy-start.2 = (s32[128]{0:T(128)S(1)}, s32[128]{0:T(128)}, u32[]{:S(2)}) copy-start(s32[128]{0:T(128)} %param.9) | copy-start | bytes 1540
  162.9 7.1 %copy-start.3 = (s32[128]{0:T(128)S(1)}, s32[128]{0:T(128)}, u32[]{:S(2)}) copy-start(s32[128]{0:T(128)} %param.8) | copy-start | bytes 1540
  162.9 100.1 %all-to-all-start = ((bf16[2,64,128,256]{2,1,0,3:T(8,128)(2,1)}), bf16[2,64,128,256]{2,1,0,3:T(8,128)(2,1)}, u32[]{:S(2)}, u32[]{:S(2)}) async-start(bf16[2,64,128,256]{2,1,0,3:T(8,128)(2,1)} %copy.19), calls=%async_computation | async-start | bytes 16777216 | tf_op jit(solution)/shard_map/all_to_all | solution.py:97
  424.6 7.1 %copy-start.4 = (s32[256]{0:T(256)S(1)}, s32[256]{0:T(256)}, u32[]{:S(2)}) copy-start(s32[256]{0:T(256)} %param.7) | copy-start | bytes 3076
  424.6 99.2 %all-to-all-start.1 = ((bf16[2,128,128,128]{3,2,0,1:T(8,128)(2,1)}), bf16[2,128,128,128]{3,2,0,1:T(8,128)(2,1)}, u32[]{:S(2)}, u32[]{:S(2)}) async-start(bf16[2,128,128,128]{3,2,0,1:T(8,128)(2,1)} %copy.22), calls=%async_computation.1 | async-start | bytes 16777216 | tf_op jit(solution)/shard_map/all_to_all | solution.py:99
  431.7 204.6 %all-gather.5.cloned.1.call-start = ((), (), s32[]{:S(2)}) async-start(), calls=%async_computation.3 | async-start | bytes 8912896 | tf_op jit(solution)/shard_map/all_gather | solution.py:106
  636.3 7.0 %copy-start = (bf16[64,128,256]{2,1,0:T(8,128)(2,1)S(1)}, bf16[64,128,256]{2,1,0:T(8,128)(2,1)}, u32[]{:S(2)}) copy-start(bf16[64,128,256]{2,1,0:T(8,128)(2,1)} %squeeze.34) | copy-start | bytes 12582916
  636.3 8.8 %copy-start.1 = (bf16[64,128,256]{2,1,0:T(8,128)(2,1)S(1)}, bf16[64,128,256]{2,1,0:T(8,128)(2,1)}, u32[]{:S(2)}) copy-start(bf16[64,128,256]{2,1,0:T(8,128)(2,1)} %squeeze.35) | copy-start | bytes 12582916
Sparse Core Ops, SparseCore 0:
  28.6 80.4 all-gather.2
  561.3 74.9 all-gather.4
where the time goes:
time: 705 us; the launch traced here: 695 us
  waiting for transfers between devices  272 us (39%)
  local copies, waits for them, and re-layouts  177 us (25%)
  matrix products  167 us (24%)
  other arithmetic  50.3 us (7%)
  starting transfers between devices  14.2 us (2%)
  between operations  14 us (2%)
    all_to_all x1, waiting for transfers between devices, body(): lax.all_to_all(relaid, 'frq', split_axis=1, concat_axis=3, tiled=True)  92 us
    all_to_all x1, waiting for transfers between devices, body(): lax.all_to_all(cross_spec, 'frq', split_axis=3, concat_axis=1, tiled=True)  88.8 us
    dot_general x4, matrix products, recompress(): jnp.dot(forward, squashed, preferred_element_type=jnp.float32)  55.5 us
    unnamed x13, local copies, waits for them, and re-layouts  50.8 us
    all_gather x1, waiting for transfers between devices, body(): lax.all_gather(ref_terms.astype(jnp.bfloat16), 'rcv', axis=3, tiled=True)  45.7 us
    all_gather x1, waiting for transfers between devices, body(): lax.all_gather(selected.astype(jnp.bfloat16), 'rcv', axis=3, tiled=True)  45.3 us
    dot_general x4, matrix products, recompress(): series = jnp.dot(inverse, flattened, preferred_element_type=jnp.float32)  38.9 us
    all_to_all x2, local copies, waits for them, and re-layouts, body(): lax.all_to_all(relaid, 'frq', split_axis=1, concat_axis=3, tiled=True)  30.8 us
  transfers between devices with their start and end apart: 4, of which 4 were waited for; matrix products, arithmetic and copies ran while one was open for 10% of the time, Pallas kernels for 0%

commit v1 on v0

v1 whole, which is shorter than its diff:
```python
import functools
import math

import jax
import jax.numpy as jnp
from jax import lax
from jax.experimental import pallas as pl
from jax.experimental.pallas import tpu as pltpu
from jax.sharding import PartitionSpec as P


L = 1024
FIRST_LAG = L // 16
LANES = 128
QUAD = 4


NT = (((1,), (1,)), ((), ()))


def in_hbm(arrays):
    return [pltpu.with_memory_space_constraint(a, pltpu.MemorySpace.HBM) for a in arrays]


def used_lags():
    ahead = jnp.arange(FIRST_LAG, L // 2, dtype=jnp.int32)
    return jnp.concatenate([ahead, L - ahead])


def lag_tables(freq_total, freq_ids_in, freq_ids_out):
    lags = used_lags()

    def tables(freq_ids):
        steps = (freq_ids[:, None] + 1) * lags[None, :] % L
        angles = steps.astype(jnp.float32) * (2.0 * math.pi / L)
        return jnp.cos(angles), jnp.sin(angles)

    cosine, sine = tables(freq_ids_in.reshape(-1))
    shape = freq_ids_in.shape + (lags.shape[0],)
    stacked = jnp.stack([cosine.reshape(shape), -sine.reshape(shape)], axis=1)
    stacked = stacked.reshape(-1, lags.shape[0])
    inverse = (stacked.T * (1.0 / math.sqrt(freq_total))).astype(jnp.bfloat16)
    cosine, sine = tables(freq_ids_out)
    forward = jnp.concatenate([cosine, -sine], axis=0)
    forward = (forward * (4.0 / math.sqrt(L))).astype(jnp.bfloat16)
    return inverse, forward


def taper_at(first, last):
    reach = jnp.arange(FIRST_LAG, L // 2, dtype=jnp.int32)[:, None]
    first = first[..., None, :]
    last = last[..., None, :]
    inside = (reach >= first) & (reach < last)
    span = (last - first).astype(jnp.float32)
    value = jnp.sin(math.pi * ((reach - first).astype(jnp.float32) + 0.5) / span)
    return jnp.where(inside, value * value, jnp.zeros_like(value))


def select_kernel(windows, fb, x_ref, onehot_ref, xf_ref, s_ref):
    for c in range(2):
        xf_ref[:, c * windows : (c + 1) * windows, :] = jnp.swapaxes(x_ref[c], 0, 1)
    for f in range(fb):
        picked = lax.dot_general(
            onehot_ref[...], xf_ref[f], NT, preferred_element_type=jnp.float32
        )
        s_ref[f] = picked.astype(jnp.bfloat16)


def select_sources(spectra, onehot, part, parts):
    _, windows, freqs, rcvs = spectra.shape
    freqs //= parts
    count = onehot.shape[0]
    fb = min(freqs, 16)
    first = part * freqs // fb
    return pl.pallas_call(
        functools.partial(select_kernel, windows, fb),
        grid=(freqs // fb,),
        in_specs=[
            pl.BlockSpec((2, windows, fb, rcvs), lambda i: (0, 0, first + i, 0)),
            pl.BlockSpec((count, rcvs), lambda i: (0, 0)),
        ],
        out_specs=[
            pl.BlockSpec((fb, 2 * windows, rcvs), lambda i: (i, 0, 0)),
            pl.BlockSpec((fb, count, 2 * windows), lambda i: (i, 0, 0)),
        ],
        out_shape=[
            jax.ShapeDtypeStruct((freqs, 2 * windows, rcvs), spectra.dtype),
            jax.ShapeDtypeStruct((freqs, count, 2 * windows), spectra.dtype),
        ],
        compiler_params=pltpu.CompilerParams(vmem_limit_bytes=50 << 20),
        name="select",
    )(spectra, onehot)


def cross_kernel(windows, fb, steps, planes, halves, scale, *refs):
    parts, shards = len(steps), planes * QUAD
    inputs, sources = refs[:parts], refs[parts : parts + shards]
    outs, held = refs[parts + shards : -1], refs[-1]

    def multiply(x_ref):
        for f in range(fb):
            a = jnp.concatenate([s[f] for s in sources], axis=0)
            turned = jnp.concatenate([-a[:, windows:], a[:, :windows]], axis=1)
            left = jnp.concatenate([a, turned], axis=0)
            product = jnp.dot(left, x_ref[f], preferred_element_type=jnp.float32)
            product = (product * scale).astype(jnp.bfloat16)
            count = a.shape[0]
            held[0, f] = product[:count]
            held[1, f] = product[count:]

    if parts == 1:
        multiply(inputs[0])
    else:
        step = pl.program_id(0)
        first = 0
        for count, x_ref in zip(steps, inputs):
            pl.when((step >= first) & (step < first + count))(
                functools.partial(multiply, x_ref)
            )
            first += count
    total = held.shape[2] // planes
    for c in range(2):
        swapped = jnp.swapaxes(held[c], 0, 1)
        for k in range(planes):
            for h in range(halves):
                outs[k * halves + h][:, c] = swapped[
                    k * total : (k + 1) * total, :, h * LANES : (h + 1) * LANES
                ]


def cross_spectra(by_freq, planes):
    _, depth, rcvs = by_freq[0].shape
    sources = [shard for plane in planes for shard in plane]
    count = sources[0].shape[1]
    total = QUAD * count
    halves = rcvs // LANES
    fb = min(16, *[x.shape[0] for x in by_freq]) if len(by_freq) > 1 else min(16, by_freq[0].shape[0])
    steps = [x.shape[0] // fb for x in by_freq]
    freqs = sum(steps) * fb
    arrays = len(planes) * halves

    def x_spec(part):
        first = sum(steps[:part])
        return pl.BlockSpec(
            (fb, depth, rcvs), lambda i: (jnp.clip(i - first, 0, steps[part] - 1), 0, 0)
        )

    blocks = pl.pallas_call(
        functools.partial(
            cross_kernel, depth // 2, fb, steps, len(planes), halves, 1.0 / math.sqrt(depth // 2)
        ),
        grid=(sum(steps),),
        in_specs=[x_spec(part) for part in range(len(by_freq))]
        + [pl.BlockSpec((fb, count, depth), lambda i: (i, 0, 0))] * len(sources),
        out_specs=[pl.BlockSpec((total, 2, fb, LANES), lambda i: (0, 0, i, 0))] * arrays,
        out_shape=[pltpu.HBM((total, 2, freqs, LANES), jnp.bfloat16)] * arrays,
        scratch_shapes=[pltpu.VMEM((2, fb, len(planes) * total, rcvs), jnp.bfloat16)],
        compiler_params=pltpu.CompilerParams(vmem_limit_bytes=50 << 20),
        name="cross",
    )(*by_freq, *sources)
    blocks = [t.reshape(total, 2 * freqs, LANES) for t in blocks]
    return [blocks[k * halves : (k + 1) * halves] for k in range(len(planes))]


def squashed_transform(inverse_ref, forward_ref, spectrum, weights_of):
    lag_count = inverse_ref.shape[0]
    result = None
    for start in range(0, lag_count, 256):
        stop = min(start + 256, lag_count)
        series = jnp.dot(
            inverse_ref[start:stop, :], spectrum, preferred_element_type=jnp.float32
        )
        x = series * weights_of(start, stop)
        squashed = (x * lax.rsqrt(1.0 + x * x)).astype(jnp.bfloat16)
        part = jnp.dot(
            forward_ref[:, start:stop], squashed, preferred_element_type=jnp.float32
        )
        result = part if result is None else result + part
    return result.astype(jnp.bfloat16)


def rows_of(table, start, stop):
    half = table.shape[0]
    pieces = []
    while start < stop:
        at = start % half
        size = min(stop - start, half - at)
        pieces.append(table[at : at + size])
        start += size
    return pieces[0] if len(pieces) == 1 else jnp.concatenate(pieces, axis=0)


def column_of(blocks, parts, index):
    if parts == 1:
        return jnp.concatenate([b[index] for b in blocks], axis=0)
    rows = []
    for peer in range(0, len(blocks), parts):
        for c in range(2):
            for b in blocks[peer : peer + parts]:
                half = b.shape[1] // 2
                rows.append(b[index, c * half : (c + 1) * half, :])
    return jnp.concatenate(rows, axis=0)


def recompress_kernel(
    count, parts, vb, first_column, info_ref, inverse_ref, forward_ref, taper_ref, *refs
):
    blocks, out_ref, held = refs[:count], refs[count], refs[count + 1]
    step = pl.program_id(0)
    columns = taper_ref.shape[1]
    freqs = out_ref.shape[0]

    def pair(i, carry):
        v = 2 * i
        spectrum = jnp.concatenate(
            [column_of(blocks, parts, v), column_of(blocks, parts, v + 1)], axis=1
        )
        at = first_column + step * vb + v
        turned = pltpu.roll(taper_ref[...], columns - at, 1)
        lanes = (turned.shape[0], LANES)
        weights = jnp.concatenate(
            [
                jnp.broadcast_to(turned[:, 0:1], lanes),
                jnp.broadcast_to(turned[:, 1:2], lanes),
            ],
            axis=1,
        )
        result = squashed_transform(
            inverse_ref, forward_ref, spectrum, lambda a, b: rows_of(weights, a, b)
        )
        row = info_ref[step] + v
        held[row] = result[:, :LANES]
        held[row + 1] = result[:, LANES:]
        return carry

    lax.fori_loop(0, vb // 2, pair, 0, unroll=True)

    @pl.when(step == pl.num_programs(0) - 1)
    def _():
        for c in range(2):
            out_ref[:, c] = jnp.swapaxes(held[:, c * freqs : (c + 1) * freqs, :], 0, 1)


def recompress(pieces, parts, inverse, forward, taper, first_column, info):
    total, part_rows, _ = pieces[0].shape
    rows = part_rows * parts
    vb = total // QUAD
    lag_count, depth = inverse.shape
    freqs = rows // 2
    fixed = lambda i, info_ref: (0, 0)
    return pl.pallas_call(
        functools.partial(recompress_kernel, len(pieces), parts, vb, first_column),
        grid_spec=pltpu.PrefetchScalarGridSpec(
            num_scalar_prefetch=1,
            grid=(QUAD,),
            in_specs=[
                pl.BlockSpec((lag_count, depth), fixed),
                pl.BlockSpec((rows, lag_count), fixed),
                pl.BlockSpec(taper.shape, fixed),
            ]
            + [pl.BlockSpec((vb, part_rows, LANES), lambda i, info_ref: (i, 0, 0))] * len(pieces),
            out_specs=pl.BlockSpec(
                (freqs, 2, total, LANES), lambda i, info_ref: (0, 0, 0, 0)
            ),
            scratch_shapes=[pltpu.VMEM((total, rows, LANES), jnp.bfloat16)],
        ),
        out_shape=pltpu.HBM((freqs, 2, total, LANES), jnp.bfloat16),
        compiler_params=pltpu.CompilerParams(vmem_limit_bytes=50 << 20),
        name="recompress",
    )(info, inverse, forward, taper, *in_hbm(pieces))


def reference_kernel(halves, parts, per_source, lanes_ref, *refs):
    blocks, out_ref = refs[:-1], refs[-1]
    rcvs = halves * LANES
    columns = out_ref.shape[2]
    share = columns // per_source
    rows = lax.broadcasted_iota(jnp.int32, (rcvs, columns), 0)
    group = lax.broadcasted_iota(jnp.int32, (rcvs, columns), 1) // share
    hit = rows == lanes_ref[...]
    results = [None] * parts
    for j in range(per_source):
        onehot = jnp.where(hit & (group == j), 1.0, 0.0).astype(jnp.bfloat16)
        for p in range(parts):
            own = blocks[p * halves : (p + 1) * halves]
            left = jnp.concatenate([b[j] for b in own], axis=1)
            found = jnp.dot(left, onehot, preferred_element_type=jnp.float32)
            results[p] = found if j == 0 else results[p] + found
    size = results[0].shape[0] // 2
    for c in range(2):
        for p in range(parts):
            row = (c * parts + p) * size
            out_ref[0, row : row + size] = results[p][c * size : (c + 1) * size].astype(
                jnp.bfloat16
            )


def reference_columns(pieces, parts, ref_lanes, per_source):
    total, part_rows, _ = pieces[0].shape
    rows = part_rows * parts
    columns = ref_lanes.shape[1]
    halves = len(pieces) // parts
    return pl.pallas_call(
        functools.partial(reference_kernel, halves, parts, per_source),
        grid=(total // per_source,),
        in_specs=[pl.BlockSpec(ref_lanes.shape, lambda i: (0, 0))]
        + [pl.BlockSpec((per_source, part_rows, LANES), lambda i: (i, 0, 0))] * len(pieces),
        out_specs=pl.BlockSpec((1, rows, columns), lambda i: (i, 0, 0)),
        out_shape=jax.ShapeDtypeStruct((total // per_source, rows, columns), jnp.bfloat16),
        compiler_params=pltpu.CompilerParams(vmem_limit_bytes=50 << 20),
        name="refcols",
    )(ref_lanes, *in_hbm(pieces))


def reference_recompress_kernel(
    peers, per_step, per_source, info_ref, inverse_ref, forward_ref, parts_ref, *refs
):
    blocks, out_ref = refs[:peers], refs[peers]
    step = pl.program_id(0)
    columns = out_ref.shape[2]
    share = columns // per_source
    spectrum = jnp.concatenate(
        [jnp.concatenate([b[u] for b in blocks], axis=0) for u in range(per_step)], axis=1
    )
    sources = parts_ref.shape[1] // 3
    shape = (sources, per_step * columns)
    wanted = step * per_step * per_source + lax.broadcasted_iota(jnp.int32, shape, 1) // share
    pick = jnp.where(lax.broadcasted_iota(jnp.int32, shape, 0) == wanted, 1.0, 0.0)
    pick = pick.astype(jnp.bfloat16)
    weights = jnp.dot(
        parts_ref[...],
        jnp.concatenate([pick] * 3, axis=0),
        preferred_element_type=jnp.float32,
    )
    result = squashed_transform(
        inverse_ref, forward_ref, spectrum, lambda a, b: rows_of(weights, a, b)
    )
    for u in range(per_step):
        out_ref[info_ref[step * per_step + u]] = result[:, u * columns : (u + 1) * columns]


def in_parts(values):
    parts, rest = [], values
    for _ in range(3):
        part = lax.reduce_precision(rest, exponent_bits=8, mantissa_bits=7)
        parts.append(part.astype(jnp.bfloat16))
        rest = rest - part
    return jnp.concatenate(parts, axis=1)


def reference_recompress(pieces, inverse, forward, parts, devices, per_source):
    slots, rows, columns = pieces[0].shape
    lag_count, depth = inverse.shape
    peers = len(pieces)
    per_step = 2
    fixed = lambda i, info_ref: (0, 0)
    return pl.pallas_call(
        functools.partial(reference_recompress_kernel, peers, per_step, per_source),
        grid_spec=pltpu.PrefetchScalarGridSpec(
            num_scalar_prefetch=1,
            grid=(slots // per_step,),
            in_specs=[
                pl.BlockSpec((lag_count, depth), fixed),
                pl.BlockSpec((rows, lag_count), fixed),
                pl.BlockSpec(parts.shape, fixed),
            ]
            + [pl.BlockSpec((per_step, rows, columns), lambda i, info_ref: (i, 0, 0))] * peers,
            out_specs=pl.BlockSpec((slots, rows, columns), lambda i, info_ref: (0, 0, 0)),
        ),
        out_shape=jax.ShapeDtypeStruct((slots, rows, columns), jnp.bfloat16),
        compiler_params=pltpu.CompilerParams(vmem_limit_bytes=50 << 20),
        name="refpass",
    )(devices, inverse, forward, parts, *pieces)


def recorrelate_kernel(planes, halves, fb, scale, info_ref, *refs):
    relayed = refs[: planes * halves]
    picked = refs[planes * halves : -3]
    out_ref, left, right = refs[-3:]
    per_device = picked[0].shape[1]
    sources = relayed[0].shape[2]
    for k in range(planes):
        for c in range(2):
            row = pl.multiple_of(
                c * planes * sources + info_ref[k * QUAD] // QUAD * sources, sources
            )
            for f in range(fb):
                for h in range(halves):
                    right[f, pl.ds(row, sources), h * LANES : (h + 1) * LANES] = relayed[
                        h * planes + k
                    ][f, c]
    for slot in range(planes * QUAD):
        row = pl.multiple_of(info_ref[slot] * per_device, per_device)
        for f in range(fb):
            left[f, pl.ds(row, per_device), :] = picked[slot][f].astype(left.dtype)
    for f in range(fb):
        p = left[f].astype(jnp.bfloat16)
        half = p.shape[1] // 2
        turned = jnp.concatenate([-p[:, half:], p[:, :half]], axis=1)
        r = right[f]
        out_ref[0, f] = jnp.dot(p, r, preferred_element_type=jnp.float32) * scale
        out_ref[1, f] = jnp.dot(turned, r, preferred_element_type=jnp.float32) * scale


def recorrelate(relayed, picked, devices):
    halves, planes = len(relayed), len(relayed[0])
    relayed = [r for half in relayed for r in half]
    freqs, _, sources, _ = relayed[0].shape
    per_device, depth = picked[0].shape[1:]
    fb = min(freqs, 8)
    refs_total = per_device * len(picked)
    rcvs = halves * LANES
    left_type = jnp.bfloat16 if per_device % 16 == 0 else jnp.float32
    return pl.pallas_call(
        functools.partial(
            recorrelate_kernel, planes, halves, fb, 1.0 / math.sqrt(planes * sources)
        ),
        grid_spec=pltpu.PrefetchScalarGridSpec(
            num_scalar_prefetch=1,
            grid=(freqs // fb,),
            in_specs=[
                pl.BlockSpec((fb, 2, sources, LANES), lambda i, info_ref: (i, 0, 0, 0))
            ]
            * len(relayed)
            + [pl.BlockSpec((fb, per_device, depth), lambda i, info_ref: (i, 0, 0))]
            * len(picked),
            out_specs=pl.BlockSpec(
                (2, fb, refs_total, rcvs), lambda i, info_ref: (0, i, 0, 0)
            ),
            scratch_shapes=[
                pltpu.VMEM((fb, refs_total, depth), left_type),
                pltpu.VMEM((fb, 2 * planes * sources, rcvs), jnp.bfloat16),
            ],
        ),
        out_shape=jax.ShapeDtypeStruct((2, freqs, refs_total, rcvs), jnp.float32),
        compiler_params=pltpu.CompilerParams(vmem_limit_bytes=58 << 20),
        name="recorrelate",
    )(devices, *in_hbm(relayed), *in_hbm(picked))


def moved(value, planes, source_of):
    pairs = [(source_of(z, q), z * QUAD + q) for z in range(planes) for q in range(QUAD)]
    return lax.ppermute(value, "rcv", pairs)


def own_plane(x, planes):
    across = moved(x, planes, lambda z, q: z * QUAD + (q ^ 2))
    beside = moved(x, planes, lambda z, q: z * QUAD + (q ^ 1))
    both = moved(across, planes, lambda z, q: z * QUAD + (q ^ 1))
    return [x, beside, across, both]


def further_planes(x, planes):
    return [
        own_plane(moved(x, planes, lambda z, q: (z + k) % planes * QUAD + q), planes)
        for k in range(1, planes)
    ]


def plane_groups(planes):
    groups = [(0,), (1,), tuple(range(2, planes))]
    return [g for g in groups if g and g[0] < planes]


def body(spectra, virtual_sources, references, coda_start, coda_end):
    _, _, freqs, rcvs = spectra.shape
    rcv_index = lax.axis_index("rcv")
    rcv_total = lax.axis_size("rcv")
    frq_index = lax.axis_index("frq")
    frq_total = lax.axis_size("frq")
    planes = rcv_total // QUAD
    halves = rcvs // LANES
    first_rcv = rcv_index * rcvs
    local_rows = jnp.arange(rcvs, dtype=jnp.int32)
    per_device = virtual_sources.shape[0] // rcv_total
    ref_share = references.shape[0] // rcv_total
    own_picks = (
        lax.dynamic_slice_in_dim(virtual_sources, rcv_index * per_device, per_device) - first_rcv
    )
    onehot = (own_picks[:, None] == local_rows[None, :]).astype(jnp.bfloat16)
    parts = part_count(freqs)
    by_freq, selected = [], []
    for part in range(parts):
        found = select_sources(spectra, onehot, part, parts)
        by_freq.append(found[0])
        selected.append(found[1])

    place = jnp.arange(QUAD, dtype=jnp.int32) ^ (rcv_index % QUAD)
    plane_of = (rcv_index // QUAD + jnp.arange(planes, dtype=jnp.int32)) % planes
    devices = (plane_of[:, None] * QUAD + place[None, :]).reshape(-1)
    slot_start = coda_start.reshape(rcv_total, per_device)[devices]
    slot_end = coda_end.reshape(rcv_total, per_device)[devices]
    taper = taper_at(slot_start.reshape(-1), slot_end.reshape(-1))
    own_freqs = jnp.arange(freqs, dtype=jnp.int32)
    peers = (frq_index + jnp.arange(frq_total, dtype=jnp.int32)) % frq_total
    inverse, forward = lag_tables(
        freqs * frq_total,
        peers[:, None] * freqs + own_freqs[None, :],
        frq_index * freqs + own_freqs,
    )
    own_refs = (
        lax.dynamic_slice_in_dim(references, rcv_index * ref_share, ref_share) - first_rcv
    )
    ref_lanes = jnp.tile(own_refs, per_device)[None]

    def exchanged(value):
        pieces = [value]
        for s in range(1, frq_total):
            pairs = [((y + s) % frq_total, y) for y in range(frq_total)]
            pieces.append(lax.ppermute(value, "frq", pairs))
        return pieces

    info = place * per_device
    near = []
    for part in range(parts):
        shards = own_plane(selected[part], planes)
        near.append(cross_spectra([by_freq[part]], [shards])[0])
    whole = selected[0] if parts == 1 else jnp.concatenate(selected, axis=0)
    sources = further_planes(whole, planes)
    cross = []
    for group in plane_groups(planes)[1:]:
        cross += cross_spectra(by_freq, [sources[k - 1] for k in group])

    ref_cross = []
    for k in range(planes):
        pieces = [t for blocks in near for t in blocks] if k == 0 else cross[k - 1]
        ref_cross.append(
            reference_columns(pieces, 1 if k else parts, ref_lanes, per_device)
        )
    ref_pieces = exchanged(jnp.concatenate(ref_cross, axis=0))
    ref_relayed = reference_recompress(
        ref_pieces, inverse, forward, in_parts(taper), devices, per_device
    )
    own_picked = (
        ref_relayed.reshape(rcv_total, 2, freqs, per_device, ref_share)
        .transpose(2, 4, 1, 0, 3)
        .reshape(freqs, ref_share, 2 * rcv_total * per_device)
    )
    picked = own_plane(own_picked, planes)
    for plane in further_planes(own_picked, planes):
        picked += plane

    relayed = []
    for h in range(halves):
        row = []
        for k in range(planes):
            if k == 0:
                each = [exchanged(near[p][h]) for p in range(parts)]
                pieces = [piece for peer in zip(*each) for piece in peer]
            else:
                pieces = exchanged(cross[k - 1][h])
            row.append(
                recompress(
                    pieces,
                    1 if k else parts,
                    inverse,
                    forward,
                    taper,
                    k * QUAD * per_device,
                    info,
                )
            )
        relayed.append(row)
    return recorrelate(relayed, picked, devices)


def part_count(freqs):
    return 2 if freqs % 32 == 0 else 1


def solution(mesh):
    return jax.shard_map(
        body,
        mesh=mesh,
        in_specs=(P(None, None, "frq", "rcv"), P(), P(), P(), P()),
        out_specs=P(None, "frq", None, "rcv"),
        check_vma=False,
    )
```

time: 705 us -> 448 us (0.64)
  the two profiles are of different devices: /device:TPU:0 before, /device:TPU:25 now
where the time goes in v1:
time: 448 us; the launch traced here: 441 us
  waiting for transfers between devices  211 us (47%)
  Pallas kernels  167 us (37%)
  starting transfers between devices  44.3 us (10%)
  local copies, waits for them, and re-layouts  10.6 us (2%)
  other arithmetic  7.01 us (2%)
    ppermute x11, waiting for transfers between devices, exchanged(): pieces.append(lax.ppermute(value, 'frq', pairs))  132 us
    pallas_call x8, Pallas kernels, recompress(): pl.pallas_call(functools.partial(recompress_kernel, len(pieces), parts, v...  80 us
    ppermute x33, waiting for transfers between devices, moved(): return lax.ppermute(value, 'rcv', pairs)  79.1 us
    ppermute x33, starting transfers between devices, moved(): return lax.ppermute(value, 'rcv', pairs)  36.5 us
    pallas_call x4, Pallas kernels, cross_spectra(): pl.pallas_call(functools.partial(cross_kernel, depth // 2, fb, steps, len...  32.4 us
    pallas_call x1, Pallas kernels, recorrelate(): pl.pallas_call(functools.partial(recorrelate_kernel, planes, halves, fb,...  20 us
    pallas_call x2, Pallas kernels, select_sources(): pl.pallas_call(functools.partial(select_kernel, windows, fb), grid=(freqs...  15.1 us
    pallas_call x4, Pallas kernels, reference_columns(): pl.pallas_call(functools.partial(reference_kernel, halves, parts, per_sou...  12.2 us
  transfers between devices with their start and end apart: 44, of which 16 were waited for; matrix products, arithmetic and copies ran while one was open for 3% of the time, Pallas kernels for 32%

profile of v1, /device:TPU:25, one launch (start us, length us, event | category | flops | bytes accessed | tf_op | source)
XLA Modules:
  0.0 441.1 jit_solution(1677374773536640883)
XLA Ops:
  0.8 7.6 %select.47 = (bf16[32,512,256]{2,1,0:T(8,128)(2,1)}, bf16[32,8,512]{2,1,0:T(8,128)(2,1)S(1)}) custom-call(bf16[2,256,64,256]{3,2,1,0:T(8,128)(2,1)} %x_ref.3, bf16[8,256]{1,0:T(8,128)(2,1)S(1)} %fusion.12.onehot_ref), custom_call_target="tpu_custom_call" | custom-call | tf_op jit(solution)/shard_map/select/pallas_call | solution.py:75
  10.5 7.5 %select.46 = (bf16[32,512,256]{2,1,0:T(8,128)(2,1)}, bf16[32,8,512]{2,1,0:T(8,128)(2,1)S(1)}) custom-call(bf16[2,256,64,256]{3,2,1,0:T(8,128)(2,1)} %x_ref.3, bf16[8,256]{1,0:T(8,128)(2,1)S(1)} %fusion.12.onehot_ref), custom_call_target="tpu_custom_call" | custom-call | tf_op jit(solution)/shard_map/select/pallas_call | solution.py:75
  19.5 1.3 collective-permute-start.13
  23.4 4.9 %collective-permute-done.1.refs_3_ = bf16[32,8,512]{2,1,0:T(8,128)(2,1)S(1)} collective-permute-done((bf16[32,8,512]{2,1,0:T(8,128)(2,1)S(1)}, bf16[32,8,512]{2,1,0:T(8,128)(2,1)S(1)}, u32[]{:S(2)}, u32[]{:S(2)}) %collective-permute-start.1) | collective-permute-done | bytes 262176 | tf_op jit(solution)/shard_map/ppermute | solution.py:443
  28.3 1.7 collective-permute-start.5
  30.0 3.2 collective-permute-done.17.refs_6_
  35.4 31.3 %collective-permute-done.13.refs_2_ = bf16[64,8,512]{2,1,0:T(8,128)(2,1)S(1)} collective-permute-done((bf16[64,8,512]{2,1,0:T(8,128)(2,1)}, bf16[64,8,512]{2,1,0:T(8,128)(2,1)S(1)}, u32[]{:S(2)}, u32[]{:S(2)}) %collective-permute-start.13) | collective-permute-done | bytes 524320 | tf_op jit(solution)/shard_map/ppermute | solution.py:443
  68.3 1.4 collective-permute-start.2
  72.2 7.4 %collective-permute-done.15.refs_4_ = bf16[64,8,512]{2,1,0:T(8,128)(2,1)} collective-permute-done((bf16[64,8,512]{2,1,0:T(8,128)(2,1)S(1)}, bf16[64,8,512]{2,1,0:T(8,128)(2,1)}, u32[]{:S(2)}, u32[]{:S(2)}) %collective-permute-start.15) | collective-permute-done | bytes 524320 | tf_op jit(solution)/shard_map/ppermute | solution.py:443
  79.5 3.0 collective-permute-start.16
  82.6 8.1 %collective-permute-done.10.refs_4_ = bf16[64,8,512]{2,1,0:T(8,128)(2,1)S(1)} collective-permute-done((bf16[64,8,512]{2,1,0:T(8,128)(2,1)S(1)}, bf16[64,8,512]{2,1,0:T(8,128)(2,1)S(1)}, u32[]{:S(2)}, u32[]{:S(2)}) %collective-permute-start.10) | collective-permute-done | bytes 524320 | tf_op jit(solution)/shard_map/ppermute | solution.py:443
  90.7 1.7 collective-permute-start.11
  92.5 1.8 fusion.11
  94.3 1.9 fusion.10
  97.1 5.7 %cross.5 = (bf16[32,2,32,128]{3,2,1,0:T(8,128)(2,1)}, bf16[32,2,32,128]{3,2,1,0:T(8,128)(2,1)}) custom-call(bf16[32,512,256]{2,1,0:T(8,128)(2,1)} %get-tuple-element.22.refs_0_.refs_1_, bf16[32,8,512]{2,1,0:T(8,128)(2,1)S(1)} %get-tuple-element.23.refs_1_, bf16[32,8,512]{2,1,0:T(8,128)(2,1)S(1)} %copy-done.1, ...), custom_call_target="tpu_custom_call" | custom-call | tf_op jit(solution)/shard_map/cross/pallas_call | solution.py:148
  104.7 5.2 %cross.4 = (bf16[32,2,32,128]{3,2,1,0:T(8,128)(2,1)}, bf16[32,2,32,128]{3,2,1,0:T(8,128)(2,1)}) custom-call(bf16[32,512,256]{2,1,0:T(8,128)(2,1)} %get-tuple-element.19.refs_0_, bf16[32,8,512]{2,1,0:T(8,128)(2,1)S(1)} %get-tuple-element.20.refs_1_, bf16[32,8,512]{2,1,0:T(8,128)(2,1)S(1)} %copy-done.5, bf16[32,8,512]{2,1,0:T(8,128)(2,1)S(1)} %copy-done.3, ...), custom_call_target="tpu_custom_call" | custom-call | tf_op jit(solution)/shard_map/cross/pallas_call | solution.py:148
  110.0 3.1 refcols.4
  113.1 1.3 collective-permute-start.24
  114.5 11.2 %cross.7 = (bf16[32,2,64,128]{3,2,1,0:T(8,128)(2,1)}, bf16[32,2,64,128]{3,2,1,0:T(8,128)(2,1)}, bf16[32,2,64,128]{3,2,1,0:T(8,128)(2,1)}, bf16[32,2,64,128]{3,2,1,0:T(8,128)(2,1)}) custom-call(bf16[32,512,256]{2,1,0:T(8,128)(2,1)} %get-tuple-element.19.refs_0_, bf16[32,512,256]{2,1,0:T(8,128)(2,1)} %get-tuple-element.22.refs_0_.refs_1_, ...), custom_call_target="tpu_custom_call" | custom-call | tf_op jit(solution)/shard_map/cross/pallas_call | solution.py:148
  125.7 3.0 refcols.7
  128.7 3.0 refcols.6
  131.7 10.3 %cross.6 = (bf16[32,2,64,128]{3,2,1,0:T(8,128)(2,1)}, bf16[32,2,64,128]{3,2,1,0:T(8,128)(2,1)}) custom-call(bf16[32,512,256]{2,1,0:T(8,128)(2,1)} %get-tuple-element.19.refs_0_, bf16[32,512,256]{2,1,0:T(8,128)(2,1)} %get-tuple-element.22.refs_0_.refs_1_, bf16[64,8,512]{2,1,0:T(8,128)(2,1)S(1)} %collective-permute-done.8.refs_2_, ...), custom_call_target="tpu_custom_call" | custom-call | tf_op jit(solution)/shard_map/cross/pallas_call | solution.py:148
  142.0 3.0 refcols.5
  150.6 7.7 %collective-permute-done.28.refs_1_ = bf16[16,128,128]{2,1,0:T(8,128)(2,1)S(1)} collective-permute-done((bf16[16,128,128]{2,1,0:T(8,128)(2,1)S(1)}, bf16[16,128,128]{2,1,0:T(8,128)(2,1)S(1)}, u32[]{:S(2)}, u32[]{:S(2)}) %collective-permute-start.28) | collective-permute-done | bytes 524320 | tf_op jit(solution)/shard_map/ppermute | solution.py:510
  158.3 7.7 %refpass.1 = bf16[16,128,128]{2,1,0:T(8,128)(2,1)S(1)} custom-call(s32[16]{0:T(128)S(1)} %add.192.info_ref, bf16[896,256]{1,0:T(8,128)(2,1)S(1)} %bitcast.18, bf16[128,896]{1,0:T(8,128)(2,1)S(1)} %fusion.4.forward_ref, bf16[448,384]{1,0:T(8,128)(2,1)S(1)} %pad_maximum_fusion.1.parts_ref, bf16[16,128,128]{2,1,0:T(8,128)(2,1)S(1)} %pad_maximum_fusion.refs_0_, ...), custom_call_target="tpu_custom_call" | custom-call | tf_op jit(solution)/shard_map/refpass/pallas_call | solution.py:357
  169.6 11.3 %collective-permute-done.23.refs_2_ = bf16[32,64,128]{2,1,0:T(8,128)(2,1)} collective-permute-done((bf16[32,64,128]{2,1,0:T(8,128)(2,1)}, bf16[32,64,128]{2,1,0:T(8,128)(2,1)}, u32[]{:S(2)}, u32[]{:S(2)}) %collective-permute-start.23) | collective-permute-done | bytes 524320 | tf_op jit(solution)/shard_map/ppermute | solution.py:510
  180.9 11.2 %collective-permute-done.6.refs_2_ = bf16[32,64,128]{2,1,0:T(8,128)(2,1)} collective-permute-done((bf16[32,64,128]{2,1,0:T(8,128)(2,1)}, bf16[32,64,128]{2,1,0:T(8,128)(2,1)}, u32[]{:S(2)}, u32[]{:S(2)}) %collective-permute-start.6) | collective-permute-done | bytes 524320 | tf_op jit(solution)/shard_map/ppermute | solution.py:510
  192.4 2.2 collective-permute-start.29
  194.6 17.0 %collective-permute-done.36.refs_16_ = bf16[64,16,256]{2,1,0:T(8,128)(2,1)S(1)} collective-permute-done((bf16[64,16,256]{2,1,0:T(8,128)(2,1)S(1)}, bf16[64,16,256]{2,1,0:T(8,128)(2,1)S(1)}, u32[]{:S(2)}, u32[]{:S(2)}) %collective-permute-start.36) | collective-permute-done | bytes 524320 | tf_op jit(solution)/shard_map/ppermute | solution.py:443
  214.8 20.7 %collective-permute-done.12.refs_1_ = bf16[32,128,128]{2,1,0:T(8,128)(2,1)S(1)} collective-permute-done((bf16[32,128,128]{2,1,0:T(8,128)(2,1)}, bf16[32,128,128]{2,1,0:T(8,128)(2,1)S(1)}, u32[]{:S(2)}, u32[]{:S(2)}) %collective-permute-start.12) | collective-permute-done | bytes 1048608 | tf_op jit(solution)/shard_map/ppermute | solution.py:510
  235.8 22.2 %collective-permute-done.22.refs_1_ = bf16[32,128,128]{2,1,0:T(8,128)(2,1)S(1)} collective-permute-done((bf16[32,128,128]{2,1,0:T(8,128)(2,1)}, bf16[32,128,128]{2,1,0:T(8,128)(2,1)S(1)}, u32[]{:S(2)}, u32[]{:S(2)}) %collective-permute-start.22) | collective-permute-done | bytes 1048608 | tf_op jit(solution)/shard_map/ppermute | solution.py:510
  258.0 4.7 %collective-permute-start.41 = (bf16[64,16,256]{2,1,0:T(8,128)(2,1)S(1)}, bf16[64,16,256]{2,1,0:T(8,128)(2,1)S(1)}, u32[]{:S(2)}, u32[]{:S(2)}) collective-permute-start(bf16[64,16,256]{2,1,0:T(8,128)(2,1)S(1)} %collective-permute-done.40.refs_20_), channel_id=1, source_target_pairs={{2,0},{0,2},{6,4},{4,6},{10,8},{8,10},{14,12},{12,14},{18,16},{16,... | collective-permute-start | bytes 1572872 | tf_op jit(solution)/shard_map/ppermute | solution.py:443
  262.8 17.7 %collective-permute-done.21.refs_1_ = bf16[32,128,128]{2,1,0:T(8,128)(2,1)S(1)} collective-permute-done((bf16[32,128,128]{2,1,0:T(8,128)(2,1)}, bf16[32,128,128]{2,1,0:T(8,128)(2,1)S(1)}, u32[]{:S(2)}, u32[]{:S(2)}) %collective-permute-start.21) | collective-permute-done | bytes 1048608 | tf_op jit(solution)/shard_map/ppermute | solution.py:510
  280.7 22.2 %collective-permute-done.26.refs_1_ = bf16[32,128,128]{2,1,0:T(8,128)(2,1)S(1)} collective-permute-done((bf16[32,128,128]{2,1,0:T(8,128)(2,1)}, bf16[32,128,128]{2,1,0:T(8,128)(2,1)S(1)}, u32[]{:S(2)}, u32[]{:S(2)}) %collective-permute-start.26) | collective-permute-done | bytes 1048608 | tf_op jit(solution)/shard_map/ppermute | solution.py:510
  303.0 4.7 %collective-permute-start.37 = (bf16[64,16,256]{2,1,0:T(8,128)(2,1)S(1)}, bf16[64,16,256]{2,1,0:T(8,128)(2,1)S(1)}, u32[]{:S(2)}, u32[]{:S(2)}) collective-permute-start(bf16[64,16,256]{2,1,0:T(8,128)(2,1)S(1)} %collective-permute-done.36.refs_16_), channel_id=1, source_target_pairs={{2,0},{0,2},{6,4},{4,6},{10,8},{8,10},{14,12},{12,14},{18,16},{16,... | collective-permute-start | bytes 1572872 | tf_op jit(solution)/shard_map/ppermute | solution.py:443
  307.7 17.7 %collective-permute-done.27.refs_1_ = bf16[32,128,128]{2,1,0:T(8,128)(2,1)S(1)} collective-permute-done((bf16[32,128,128]{2,1,0:T(8,128)(2,1)}, bf16[32,128,128]{2,1,0:T(8,128)(2,1)S(1)}, u32[]{:S(2)}, u32[]{:S(2)}) %collective-permute-start.27) | collective-permute-done | bytes 1048608 | tf_op jit(solution)/shard_map/ppermute | solution.py:510
  325.7 2.8 collective-permute-start.33
  329.1 7.2 %collective-permute-done.34.refs_14_ = bf16[64,16,256]{2,1,0:T(8,128)(2,1)S(1)} collective-permute-done((bf16[64,16,256]{2,1,0:T(8,128)(2,1)S(1)}, bf16[64,16,256]{2,1,0:T(8,128)(2,1)S(1)}, u32[]{:S(2)}, u32[]{:S(2)}) %collective-permute-start.34) | collective-permute-done | bytes 524320 | tf_op jit(solution)/shard_map/ppermute | solution.py:443
  336.3 3.4 collective-permute-start.35
  339.8 10.2 %recompress.12.refs_4_ = bf16[64,2,32,128]{3,2,1,0:T(8,128)(2,1)} custom-call(s32[4]{0:T(128)S(1)} %broadcast_multiply_fusion.info_ref, bf16[896,256]{1,0:T(8,128)(2,1)S(1)} %bitcast.19, bf16[128,896]{1,0:T(8,128)(2,1)S(1)} %fusion.4.forward_ref, f32[448,128]{1,0:T(8,128)S(1)} %get-tuple-element.40.taper_ref, bf16[32,64,128]{2,1,0:T(8,128)(2,1)} %bitcast.58, ...), custom_call_target="tpu_custom_call" | custom-call | tf_op jit(solution)/shard_map/recompress/pallas_call | solution.py:251
  349.9 10.0 %recompress.8.refs_0_ = bf16[64,2,32,128]{3,2,1,0:T(8,128)(2,1)} custom-call(s32[4]{0:T(128)S(1)} %broadcast_multiply_fusion.info_ref, bf16[896,256]{1,0:T(8,128)(2,1)S(1)} %bitcast.20, bf16[128,896]{1,0:T(8,128)(2,1)S(1)} %fusion.4.forward_ref, f32[448,128]{1,0:T(8,128)S(1)} %get-tuple-element.40.taper_ref, bf16[32,64,128]{2,1,0:T(8,128)(2,1)} %bitcast.55, ...), custom_call_target="tpu_custom_call" | custom-call | tf_op jit(solution)/shard_map/recompress/pallas_call | solution.py:251
  359.9 9.9 %recompress.13.refs_5_ = bf16[64,2,32,128]{3,2,1,0:T(8,128)(2,1)} custom-call(s32[4]{0:T(128)S(1)} %broadcast_multiply_fusion.info_ref, bf16[896,256]{1,0:T(8,128)(2,1)S(1)} %bitcast.21, bf16[128,896]{1,0:T(8,128)(2,1)S(1)} %fusion.4.forward_ref, f32[448,128]{1,0:T(8,128)S(1)} %get-tuple-element.40.taper_ref, bf16[32,128,128]{2,1,0:T(8,128)(2,1)} %bitcast.46, ...), custom_call_target="tpu_custom_call" | custom-call | tf_op jit(solution)/shard_map/recompress/pallas_call | solution.py:251
  369.8 9.9 %recompress.9.refs_1_ = bf16[64,2,32,128]{3,2,1,0:T(8,128)(2,1)} custom-call(s32[4]{0:T(128)S(1)} %broadcast_multiply_fusion.info_ref, bf16[896,256]{1,0:T(8,128)(2,1)S(1)} %bitcast.22, bf16[128,896]{1,0:T(8,128)(2,1)S(1)} %fusion.4.forward_ref, f32[448,128]{1,0:T(8,128)S(1)} %get-tuple-element.40.taper_ref, bf16[32,128,128]{2,1,0:T(8,128)(2,1)} %bitcast.43, ...), custom_call_target="tpu_custom_call" | custom-call | tf_op jit(solution)/shard_map/recompress/pallas_call | solution.py:251
  379.8 9.9 %recompress.11.refs_3_ = bf16[64,2,32,128]{3,2,1,0:T(8,128)(2,1)} custom-call(s32[4]{0:T(128)S(1)} %broadcast_multiply_fusion.info_ref, bf16[896,256]{1,0:T(8,128)(2,1)S(1)} %bitcast.23, bf16[128,896]{1,0:T(8,128)(2,1)S(1)} %fusion.4.forward_ref, f32[448,128]{1,0:T(8,128)S(1)} %get-tuple-element.40.taper_ref, bf16[32,128,128]{2,1,0:T(8,128)(2,1)} %bitcast.40, ...), custom_call_target="tpu_custom_call" | custom-call | tf_op jit(solution)/shard_map/recompress/pallas_call | solution.py:251
  389.7 9.9 %recompress.10.refs_2_ = bf16[64,2,32,128]{3,2,1,0:T(8,128)(2,1)} custom-call(s32[4]{0:T(128)S(1)} %broadcast_multiply_fusion.info_ref, bf16[896,256]{1,0:T(8,128)(2,1)S(1)} %bitcast.24, bf16[128,896]{1,0:T(8,128)(2,1)S(1)} %fusion.4.forward_ref, f32[448,128]{1,0:T(8,128)S(1)} %get-tuple-element.40.taper_ref, bf16[32,128,128]{2,1,0:T(8,128)(2,1)} %bitcast.37, ...), custom_call_target="tpu_custom_call" | custom-call | tf_op jit(solution)/shard_map/recompress/pallas_call | solution.py:251
  399.6 10.2 %recompress.14.refs_6_ = bf16[64,2,32,128]{3,2,1,0:T(8,128)(2,1)} custom-call(s32[4]{0:T(128)S(1)} %broadcast_multiply_fusion.info_ref, bf16[896,256]{1,0:T(8,128)(2,1)S(1)} %bitcast.25, bf16[128,896]{1,0:T(8,128)(2,1)S(1)} %fusion.4.forward_ref, f32[448,128]{1,0:T(8,128)S(1)} %get-tuple-element.40.taper_ref, bf16[32,128,128]{2,1,0:T(8,128)(2,1)} %bitcast.34, ...), custom_call_target="tpu_custom_call" | custom-call | tf_op jit(solution)/shard_map/recompress/pallas_call | solution.py:251
  409.8 10.0 %recompress.15.refs_7_ = bf16[64,2,32,128]{3,2,1,0:T(8,128)(2,1)} custom-call(s32[4]{0:T(128)S(1)} %broadcast_multiply_fusion.info_ref, bf16[896,256]{1,0:T(8,128)(2,1)S(1)} %bitcast.26, bf16[128,896]{1,0:T(8,128)(2,1)S(1)} %fusion.4.forward_ref, f32[448,128]{1,0:T(8,128)S(1)} %get-tuple-element.40.taper_ref, bf16[32,128,128]{2,1,0:T(8,128)(2,1)} %bitcast.31, ...), custom_call_target="tpu_custom_call" | custom-call | tf_op jit(solution)/shard_map/recompress/pallas_call | solution.py:251
  420.8 20.0 %recorrelate.1 = f32[2,64,256,256]{3,2,1,0:T(8,128)} custom-call(s32[16]{0:T(128)} %copy-done.6, bf16[64,2,32,128]{3,2,1,0:T(8,128)(2,1)} %recompress.8.refs_0_, bf16[64,2,32,128]{3,2,1,0:T(8,128)(2,1)} %recompress.9.refs_1_, bf16[64,2,32,128]{3,2,1,0:T(8,128)(2,1)} %recompress.10.refs_2_, bf16[64,2,32,128]{3,2,1,0:T(8,128)(2,1)} %recompress.11.refs_3_, ...), custom_call_target="tpu_custom_call" | custom-call | tf_op jit(solution)/shard_map/recorrelate/pallas_call | solution.py:414
  (158 shorter events, 31.1 us)
Async XLA Ops:
  8.4 12.8 %collective-permute-start.4 = (bf16[32,8,512]{2,1,0:T(8,128)(2,1)S(1)}, bf16[32,8,512]{2,1,0:T(8,128)(2,1)S(1)}, u32[]{:S(2)}, u32[]{:S(2)}) collective-permute-start(bf16[32,8,512]{2,1,0:T(8,128)(2,1)S(1)} %get-tuple-element.23.refs_1_), channel_id=1, source_target_pairs={{4,0},{6,2},{0,4},{2,6},{12,8},{14,10},{8,12},{10,14},{20,16},{22,... | collective-permute-start | bytes 786440 | tf_op jit(solution)/shard_map/ppermute | solution.py:443
  9.6 12.0 %collective-permute-start.3 = (bf16[32,8,512]{2,1,0:T(8,128)(2,1)S(1)}, bf16[32,8,512]{2,1,0:T(8,128)(2,1)S(1)}, u32[]{:S(2)}, u32[]{:S(2)}) collective-permute-start(bf16[32,8,512]{2,1,0:T(8,128)(2,1)S(1)} %get-tuple-element.23.refs_1_), channel_id=1, source_target_pairs={{2,0},{0,2},{6,4},{4,6},{10,8},{8,10},{14,12},{12,14},{18,16},{16,... | collective-permute-start | bytes 786440 | tf_op jit(solution)/shard_map/ppermute | solution.py:443
  19.5 13.7 %collective-permute-start.17 = (bf16[64,8,512]{2,1,0:T(8,128)(2,1)}, bf16[64,8,512]{2,1,0:T(8,128)(2,1)S(1)}, u32[]{:S(2)}, u32[]{:S(2)}) collective-permute-start(bf16[64,8,512]{2,1,0:T(8,128)(2,1)} %constant_dynamic-update-slice_fusion), channel_id=1, source_target_pairs={{24,0},{26,2},{28,4},{30,6},{0,8},{2,10},{4,12},{6,14},{8,16},{10,... | collective-permute-start | bytes 1572872 | tf_op jit(solution)/shard_map/ppermute | solution.py:443
  19.5 47.3 %collective-permute-start.13 = (bf16[64,8,512]{2,1,0:T(8,128)(2,1)}, bf16[64,8,512]{2,1,0:T(8,128)(2,1)S(1)}, u32[]{:S(2)}, u32[]{:S(2)}) collective-permute-start(bf16[64,8,512]{2,1,0:T(8,128)(2,1)} %constant_dynamic-update-slice_fusion), channel_id=1, source_target_pairs={{16,0},{18,2},{20,4},{22,6},{24,8},{26,10},{28,12},{30,14},{0,16},... | collective-permute-start | bytes 1572872 | tf_op jit(solution)/shard_map/ppermute | solution.py:443
  20.9 46.2 %collective-permute-start.8 = (bf16[64,8,512]{2,1,0:T(8,128)(2,1)}, bf16[64,8,512]{2,1,0:T(8,128)(2,1)S(1)}, u32[]{:S(2)}, u32[]{:S(2)}) collective-permute-start(bf16[64,8,512]{2,1,0:T(8,128)(2,1)} %constant_dynamic-update-slice_fusion), channel_id=1, source_target_pairs={{8,0},{10,2},{12,4},{14,6},{16,8},{18,10},{20,12},{22,14},{24,16},... | collective-permute-start | bytes 1572872 | tf_op jit(solution)/shard_map/ppermute | solution.py:443
  21.2 7.1 %collective-permute-start.1 = (bf16[32,8,512]{2,1,0:T(8,128)(2,1)S(1)}, bf16[32,8,512]{2,1,0:T(8,128)(2,1)S(1)}, u32[]{:S(2)}, u32[]{:S(2)}) collective-permute-start(bf16[32,8,512]{2,1,0:T(8,128)(2,1)S(1)} %get-tuple-element.20.refs_1_), channel_id=1, source_target_pairs={{4,0},{6,2},{0,4},{2,6},{12,8},{14,10},{8,12},{10,14},{20,16},{22,... | collective-permute-start | bytes 786440 | tf_op jit(solution)/shard_map/ppermute | solution.py:443
  22.2 11.2 %collective-permute-start = (bf16[32,8,512]{2,1,0:T(8,128)(2,1)S(1)}, bf16[32,8,512]{2,1,0:T(8,128)(2,1)S(1)}, u32[]{:S(2)}, u32[]{:S(2)}) collective-permute-start(bf16[32,8,512]{2,1,0:T(8,128)(2,1)S(1)} %get-tuple-element.20.refs_1_), channel_id=1, source_target_pairs={{2,0},{0,2},{6,4},{4,6},{10,8},{8,10},{14,12},{12,14},{18,16},{16,... | collective-permute-start | bytes 786440 | tf_op jit(solution)/shard_map/ppermute | solution.py:443
  28.3 40.0 %collective-permute-start.5 = (bf16[32,8,512]{2,1,0:T(8,128)(2,1)S(1)}, bf16[32,8,512]{2,1,0:T(8,128)(2,1)}, u32[]{:S(2)}, u32[]{:S(2)}) collective-permute-start(bf16[32,8,512]{2,1,0:T(8,128)(2,1)S(1)} %collective-permute-done.4.refs_3_), channel_id=1, source_target_pairs={{2,0},{0,2},{6,4},{4,6},{10,8},{8,10},{14,12},{12,14},{18,16},{16,... | collective-permute-start | bytes 786440 | tf_op jit(solution)/shard_map/ppermute | solution.py:443
  33.2 38.4 %collective-permute-start.19 = (bf16[64,8,512]{2,1,0:T(8,128)(2,1)S(1)}, bf16[64,8,512]{2,1,0:T(8,128)(2,1)S(1)}, u32[]{:S(2)}, u32[]{:S(2)}) collective-permute-start(bf16[64,8,512]{2,1,0:T(8,128)(2,1)S(1)} %collective-permute-done.17.refs_6_), channel_id=1, source_target_pairs={{4,0},{6,2},{0,4},{2,6},{12,8},{14,10},{8,12},{10,14},{20,16},{22,... | collective-permute-start | bytes 1572872 | tf_op jit(solution)/shard_map/ppermute | solution.py:443
  34.2 37.7 %collective-permute-start.18 = (bf16[64,8,512]{2,1,0:T(8,128)(2,1)S(1)}, bf16[64,8,512]{2,1,0:T(8,128)(2,1)}, u32[]{:S(2)}, u32[]{:S(2)}) collective-permute-start(bf16[64,8,512]{2,1,0:T(8,128)(2,1)S(1)} %collective-permute-done.17.refs_6_), channel_id=1, source_target_pairs={{2,0},{0,2},{6,4},{4,6},{10,8},{8,10},{14,12},{12,14},{18,16},{16,... | collective-permute-start | bytes 1572872 | tf_op jit(solution)/shard_map/ppermute | solution.py:443
  66.8 12.7 %collective-permute-start.15 = (bf16[64,8,512]{2,1,0:T(8,128)(2,1)S(1)}, bf16[64,8,512]{2,1,0:T(8,128)(2,1)}, u32[]{:S(2)}, u32[]{:S(2)}) collective-permute-start(bf16[64,8,512]{2,1,0:T(8,128)(2,1)S(1)} %collective-permute-done.13.refs_2_), channel_id=1, source_target_pairs={{4,0},{6,2},{0,4},{2,6},{12,8},{14,10},{8,12},{10,14},{20,16},{22,... | collective-permute-start | bytes 1572872 | tf_op jit(solution)/shard_map/ppermute | solution.py:443
  67.1 23.6 %collective-permute-start.10 = (bf16[64,8,512]{2,1,0:T(8,128)(2,1)S(1)}, bf16[64,8,512]{2,1,0:T(8,128)(2,1)S(1)}, u32[]{:S(2)}, u32[]{:S(2)}) collective-permute-start(bf16[64,8,512]{2,1,0:T(8,128)(2,1)S(1)} %collective-permute-done.8.refs_2_), channel_id=1, source_target_pairs={{4,0},{6,2},{0,4},{2,6},{12,8},{14,10},{8,12},{10,14},{20,16},{22,... | collective-permute-start | bytes 1572872 | tf_op jit(solution)/shard_map/ppermute | solution.py:443
  68.3 2.9 collective-permute-start.2
  71.3 41.8 %collective-permute-start.14 = (bf16[64,8,512]{2,1,0:T(8,128)(2,1)S(1)}, bf16[64,8,512]{2,1,0:T(8,128)(2,1)}, u32[]{:S(2)}, u32[]{:S(2)}) collective-permute-start(bf16[64,8,512]{2,1,0:T(8,128)(2,1)S(1)} %collective-permute-done.13.refs_2_), channel_id=1, source_target_pairs={{2,0},{0,2},{6,4},{4,6},{10,8},{8,10},{14,12},{12,14},{18,16},{16,... | collective-permute-start | bytes 1572872 | tf_op jit(solution)/shard_map/ppermute | solution.py:443
  71.6 60.0 %collective-permute-start.9 = (bf16[64,8,512]{2,1,0:T(8,128)(2,1)S(1)}, bf16[64,8,512]{2,1,0:T(8,128)(2,1)}, u32[]{:S(2)}, u32[]{:S(2)}) collective-permute-start(bf16[64,8,512]{2,1,0:T(8,128)(2,1)S(1)} %collective-permute-done.8.refs_2_), channel_id=1, source_target_pairs={{2,0},{0,2},{6,4},{4,6},{10,8},{8,10},{14,12},{12,14},{18,16},{16,... | collective-permute-start | bytes 1572872 | tf_op jit(solution)/shard_map/ppermute | solution.py:443
  71.9 42.6 %collective-permute-start.20 = (bf16[64,8,512]{2,1,0:T(8,128)(2,1)S(1)}, bf16[64,8,512]{2,1,0:T(8,128)(2,1)}, u32[]{:S(2)}, u32[]{:S(2)}) collective-permute-start(bf16[64,8,512]{2,1,0:T(8,128)(2,1)S(1)} %collective-permute-done.19.refs_8_), channel_id=1, source_target_pairs={{2,0},{0,2},{6,4},{4,6},{10,8},{8,10},{14,12},{12,14},{18,16},{16,... | collective-permute-start | bytes 1572872 | tf_op jit(solution)/shard_map/ppermute | solution.py:443
  79.5 34.9 %collective-permute-start.16 = (bf16[64,8,512]{2,1,0:T(8,128)(2,1)}, bf16[64,8,512]{2,1,0:T(8,128)(2,1)}, u32[]{:S(2)}, u32[]{:S(2)}) collective-permute-start(bf16[64,8,512]{2,1,0:T(8,128)(2,1)} %collective-permute-done.15.refs_4_), channel_id=1, source_target_pairs={{2,0},{0,2},{6,4},{4,6},{10,8},{8,10},{14,12},{12,14},{18,16},{16,... | collective-permute-start | bytes 1572872 | tf_op jit(solution)/shard_map/ppermute | solution.py:443
  90.7 41.1 %collective-permute-start.11 = (bf16[64,8,512]{2,1,0:T(8,128)(2,1)S(1)}, bf16[64,8,512]{2,1,0:T(8,128)(2,1)}, u32[]{:S(2)}, u32[]{:S(2)}) collective-permute-start(bf16[64,8,512]{2,1,0:T(8,128)(2,1)S(1)} %collective-permute-done.10.refs_4_), channel_id=1, source_target_pairs={{2,0},{0,2},{6,4},{4,6},{10,8},{8,10},{14,12},{12,14},{18,16},{16,... | collective-permute-start | bytes 1572872 | tf_op jit(solution)/shard_map/ppermute | solution.py:443
  113.1 55.0 %collective-permute-start.24 = (bf16[32,64,128]{2,1,0:T(8,128)(2,1)}, bf16[32,64,128]{2,1,0:T(8,128)(2,1)}, u32[]{:S(2)}, u32[]{:S(2)}) collective-permute-start(bf16[32,64,128]{2,1,0:T(8,128)(2,1)} %bitcast.51), channel_id=1, source_target_pairs={{1,0},{0,1},{3,2},{2,3},{5,4},{4,5},{7,6},{6,7},{9,8},{8,9},{11,10... | collective-permute-start | bytes 1572872 | tf_op jit(solution)/shard_map/ppermute | solution.py:510
  145.1 13.3 %collective-permute-start.28 = (bf16[16,128,128]{2,1,0:T(8,128)(2,1)S(1)}, bf16[16,128,128]{2,1,0:T(8,128)(2,1)S(1)}, u32[]{:S(2)}, u32[]{:S(2)}) collective-permute-start(bf16[16,128,128]{2,1,0:T(8,128)(2,1)S(1)} %pad_maximum_fusion.refs_0_), channel_id=1, source_target_pairs={{1,0},{0,1},{3,2},{2,3},{5,4},{4,5},{7,6},{6,7},{9,8},{8,9},{11,10... | collective-permute-start | bytes 1572872 | tf_op jit(solution)/shard_map/ppermute | solution.py:510
  145.5 254.1 %copy-start.6 = (s32[16]{0:T(128)}, s32[16]{0:T(128)S(1)}, u32[]{:S(2)}) copy-start(s32[16]{0:T(128)S(1)} %add.192.info_ref) | copy-start | bytes 196
  147.8 21.7 %collective-permute-start.7 = (bf16[32,64,128]{2,1,0:T(8,128)(2,1)}, bf16[32,64,128]{2,1,0:T(8,128)(2,1)S(1)}, u32[]{:S(2)}, u32[]{:S(2)}) collective-permute-start(bf16[32,64,128]{2,1,0:T(8,128)(2,1)} %bitcast.48), channel_id=1, source_target_pairs={{1,0},{0,1},{3,2},{2,3},{5,4},{4,5},{7,6},{6,7},{9,8},{8,9},{11,10... | collective-permute-start | bytes 1572872 | tf_op jit(solution)/shard_map/ppermute | solution.py:510
  149.1 31.8 %collective-permute-start.23 = (bf16[32,64,128]{2,1,0:T(8,128)(2,1)}, bf16[32,64,128]{2,1,0:T(8,128)(2,1)}, u32[]{:S(2)}, u32[]{:S(2)}) collective-permute-start(bf16[32,64,128]{2,1,0:T(8,128)(2,1)} %bitcast.57), channel_id=1, source_target_pairs={{1,0},{0,1},{3,2},{2,3},{5,4},{4,5},{7,6},{6,7},{9,8},{8,9},{11,10... | collective-permute-start | bytes 1572872 | tf_op jit(solution)/shard_map/ppermute | solution.py:510
  149.3 42.8 %collective-permute-start.6 = (bf16[32,64,128]{2,1,0:T(8,128)(2,1)}, bf16[32,64,128]{2,1,0:T(8,128)(2,1)}, u32[]{:S(2)}, u32[]{:S(2)}) collective-permute-start(bf16[32,64,128]{2,1,0:T(8,128)(2,1)} %bitcast.54), channel_id=1, source_target_pairs={{1,0},{0,1},{3,2},{2,3},{5,4},{4,5},{7,6},{6,7},{9,8},{8,9},{11,10... | collective-permute-start | bytes 1572872 | tf_op jit(solution)/shard_map/ppermute | solution.py:510
  168.0 252.7 %copy-start.7 = (bf16[64,16,256]{2,1,0:T(8,128)(2,1)}, bf16[64,16,256]{2,1,0:T(8,128)(2,1)S(1)}, u32[]{:S(2)}) copy-start(bf16[64,16,256]{2,1,0:T(8,128)(2,1)S(1)} %copy.15.refs_8_) | copy-start | bytes 1572868
  168.0 24.3 %collective-permute-start.40 = (bf16[64,16,256]{2,1,0:T(8,128)(2,1)S(1)}, bf16[64,16,256]{2,1,0:T(8,128)(2,1)S(1)}, u32[]{:S(2)}, u32[]{:S(2)}) collective-permute-start(bf16[64,16,256]{2,1,0:T(8,128)(2,1)S(1)} %copy.15.refs_8_), channel_id=1, source_target_pairs={{24,0},{26,2},{28,4},{30,6},{0,8},{2,10},{4,12},{6,14},{8,16},{10,... | collective-permute-start | bytes 1572872 | tf_op jit(solution)/shard_map/ppermute | solution.py:443
  168.1 46.4 %collective-permute-start.25 = (bf16[32,128,128]{2,1,0:T(8,128)(2,1)}, bf16[32,128,128]{2,1,0:T(8,128)(2,1)S(1)}, u32[]{:S(2)}, u32[]{:S(2)}) collective-permute-start(bf16[32,128,128]{2,1,0:T(8,128)(2,1)} %bitcast.45), channel_id=1, source_target_pairs={{1,0},{0,1},{3,2},{2,3},{5,4},{4,5},{7,6},{6,7},{9,8},{8,9},{11,10... | collective-permute-start | bytes 3145736 | tf_op jit(solution)/shard_map/ppermute | solution.py:510
  169.6 42.0 %collective-permute-start.36 = (bf16[64,16,256]{2,1,0:T(8,128)(2,1)S(1)}, bf16[64,16,256]{2,1,0:T(8,128)(2,1)S(1)}, u32[]{:S(2)}, u32[]{:S(2)}) collective-permute-start(bf16[64,16,256]{2,1,0:T(8,128)(2,1)S(1)} %copy.15.refs_8_), channel_id=1, source_target_pairs={{16,0},{18,2},{20,4},{22,6},{24,8},{26,10},{28,12},{30,14},{0,16},... | collective-permute-start | bytes 1572872 | tf_op jit(solution)/shard_map/ppermute | solution.py:443
  180.9 30.9 %collective-permute-start.32 = (bf16[64,16,256]{2,1,0:T(8,128)(2,1)S(1)}, bf16[64,16,256]{2,1,0:T(8,128)(2,1)S(1)}, u32[]{:S(2)}, u32[]{:S(2)}) collective-permute-start(bf16[64,16,256]{2,1,0:T(8,128)(2,1)S(1)} %copy.15.refs_8_), channel_id=1, source_target_pairs={{8,0},{10,2},{12,4},{14,6},{16,8},{18,10},{20,12},{22,14},{24,16},... | collective-permute-start | bytes 1572872 | tf_op jit(solution)/shard_map/ppermute | solution.py:443
  192.1 20.9 %collective-permute-start.30 = (bf16[64,16,256]{2,1,0:T(8,128)(2,1)S(1)}, bf16[64,16,256]{2,1,0:T(8,128)(2,1)S(1)}, u32[]{:S(2)}, u32[]{:S(2)}) collective-permute-start(bf16[64,16,256]{2,1,0:T(8,128)(2,1)S(1)} %copy.15.refs_8_), channel_id=1, source_target_pairs={{4,0},{6,2},{0,4},{2,6},{12,8},{14,10},{8,12},{10,14},{20,16},{22,... | collective-permute-start | bytes 1572872 | tf_op jit(solution)/shard_map/ppermute | solution.py:443
  192.4 228.4 %copy-start.14 = (bf16[64,16,256]{2,1,0:T(8,128)(2,1)}, bf16[64,16,256]{2,1,0:T(8,128)(2,1)S(1)}, u32[]{:S(2)}) copy-start(bf16[64,16,256]{2,1,0:T(8,128)(2,1)S(1)} %collective-permute-done.40.refs_20_) | copy-start | bytes 1572868
  192.4 20.9 %collective-permute-start.29 = (bf16[64,16,256]{2,1,0:T(8,128)(2,1)S(1)}, bf16[64,16,256]{2,1,0:T(8,128)(2,1)S(1)}, u32[]{:S(2)}, u32[]{:S(2)}) collective-permute-start(bf16[64,16,256]{2,1,0:T(8,128)(2,1)S(1)} %copy.15.refs_8_), channel_id=1, source_target_pairs={{2,0},{0,2},{6,4},{4,6},{10,8},{8,10},{14,12},{12,14},{18,16},{16,... | collective-permute-start | bytes 1572872 | tf_op jit(solution)/shard_map/ppermute | solution.py:443
  211.6 209.2 %copy-start.15 = (bf16[64,16,256]{2,1,0:T(8,128)(2,1)}, bf16[64,16,256]{2,1,0:T(8,128)(2,1)S(1)}, u32[]{:S(2)}) copy-start(bf16[64,16,256]{2,1,0:T(8,128)(2,1)S(1)} %collective-permute-done.36.refs_16_) | copy-start | bytes 1572868
  211.6 24.0 %collective-permute-start.12 = (bf16[32,128,128]{2,1,0:T(8,128)(2,1)}, bf16[32,128,128]{2,1,0:T(8,128)(2,1)S(1)}, u32[]{:S(2)}, u32[]{:S(2)}) collective-permute-start(bf16[32,128,128]{2,1,0:T(8,128)(2,1)} %bitcast.42), channel_id=1, source_target_pairs={{1,0},{0,1},{3,2},{2,3},{5,4},{4,5},{7,6},{6,7},{9,8},{8,9},{11,10... | collective-permute-start | bytes 3145736 | tf_op jit(solution)/shard_map/ppermute | solution.py:510
  211.8 46.2 %collective-permute-start.22 = (bf16[32,128,128]{2,1,0:T(8,128)(2,1)}, bf16[32,128,128]{2,1,0:T(8,128)(2,1)S(1)}, u32[]{:S(2)}, u32[]{:S(2)}) collective-permute-start(bf16[32,128,128]{2,1,0:T(8,128)(2,1)} %bitcast.39), channel_id=1, source_target_pairs={{1,0},{0,1},{3,2},{2,3},{5,4},{4,5},{7,6},{6,7},{9,8},{8,9},{11,10... | collective-permute-start | bytes 3145736 | tf_op jit(solution)/shard_map/ppermute | solution.py:510
  213.1 67.4 %collective-permute-start.21 = (bf16[32,128,128]{2,1,0:T(8,128)(2,1)}, bf16[32,128,128]{2,1,0:T(8,128)(2,1)S(1)}, u32[]{:S(2)}, u32[]{:S(2)}) collective-permute-start(bf16[32,128,128]{2,1,0:T(8,128)(2,1)} %bitcast.36), channel_id=1, source_target_pairs={{1,0},{0,1},{3,2},{2,3},{5,4},{4,5},{7,6},{6,7},{9,8},{8,9},{11,10... | collective-permute-start | bytes 3145736 | tf_op jit(solution)/shard_map/ppermute | solution.py:510
  213.3 89.6 %collective-permute-start.26 = (bf16[32,128,128]{2,1,0:T(8,128)(2,1)}, bf16[32,128,128]{2,1,0:T(8,128)(2,1)S(1)}, u32[]{:S(2)}, u32[]{:S(2)}) collective-permute-start(bf16[32,128,128]{2,1,0:T(8,128)(2,1)} %bitcast.33), channel_id=1, source_target_pairs={{1,0},{0,1},{3,2},{2,3},{5,4},{4,5},{7,6},{6,7},{9,8},{8,9},{11,10... | collective-permute-start | bytes 3145736 | tf_op jit(solution)/shard_map/ppermute | solution.py:510
  214.5 110.9 %collective-permute-start.27 = (bf16[32,128,128]{2,1,0:T(8,128)(2,1)}, bf16[32,128,128]{2,1,0:T(8,128)(2,1)S(1)}, u32[]{:S(2)}, u32[]{:S(2)}) collective-permute-start(bf16[32,128,128]{2,1,0:T(8,128)(2,1)} %bitcast.30), channel_id=1, source_target_pairs={{1,0},{0,1},{3,2},{2,3},{5,4},{4,5},{7,6},{6,7},{9,8},{8,9},{11,10... | collective-permute-start | bytes 3145736 | tf_op jit(solution)/shard_map/ppermute | solution.py:510
  235.5 90.1 %collective-permute-start.42 = (bf16[64,16,256]{2,1,0:T(8,128)(2,1)S(1)}, bf16[64,16,256]{2,1,0:T(8,128)(2,1)S(1)}, u32[]{:S(2)}, u32[]{:S(2)}) collective-permute-start(bf16[64,16,256]{2,1,0:T(8,128)(2,1)S(1)} %collective-permute-done.40.refs_20_), channel_id=1, source_target_pairs={{4,0},{6,2},{0,4},{2,6},{12,8},{14,10},{8,12},{10,14},{20,16},{22,... | collective-permute-start | bytes 1572872 | tf_op jit(solution)/shard_map/ppermute | solution.py:443
  258.0 70.5 %collective-permute-start.41 = (bf16[64,16,256]{2,1,0:T(8,128)(2,1)S(1)}, bf16[64,16,256]{2,1,0:T(8,128)(2,1)S(1)}, u32[]{:S(2)}, u32[]{:S(2)}) collective-permute-start(bf16[64,16,256]{2,1,0:T(8,128)(2,1)S(1)} %collective-permute-done.40.refs_20_), channel_id=1, source_target_pairs={{2,0},{0,2},{6,4},{4,6},{10,8},{8,10},{14,12},{12,14},{18,16},{16,... | collective-permute-start | bytes 1572872 | tf_op jit(solution)/shard_map/ppermute | solution.py:443
  280.5 48.1 %collective-permute-start.38 = (bf16[64,16,256]{2,1,0:T(8,128)(2,1)S(1)}, bf16[64,16,256]{2,1,0:T(8,128)(2,1)S(1)}, u32[]{:S(2)}, u32[]{:S(2)}) collective-permute-start(bf16[64,16,256]{2,1,0:T(8,128)(2,1)S(1)} %collective-permute-done.36.refs_16_), channel_id=1, source_target_pairs={{4,0},{6,2},{0,4},{2,6},{12,8},{14,10},{8,12},{10,14},{20,16},{22,... | collective-permute-start | bytes 1572872 | tf_op jit(solution)/shard_map/ppermute | solution.py:443
  303.0 26.1 %collective-permute-start.37 = (bf16[64,16,256]{2,1,0:T(8,128)(2,1)S(1)}, bf16[64,16,256]{2,1,0:T(8,128)(2,1)S(1)}, u32[]{:S(2)}, u32[]{:S(2)}) collective-permute-start(bf16[64,16,256]{2,1,0:T(8,128)(2,1)S(1)} %collective-permute-done.36.refs_16_), channel_id=1, source_target_pairs={{2,0},{0,2},{6,4},{4,6},{10,8},{8,10},{14,12},{12,14},{18,16},{16,... | collective-permute-start | bytes 1572872 | tf_op jit(solution)/shard_map/ppermute | solution.py:443
  325.4 10.9 %collective-permute-start.34 = (bf16[64,16,256]{2,1,0:T(8,128)(2,1)S(1)}, bf16[64,16,256]{2,1,0:T(8,128)(2,1)S(1)}, u32[]{:S(2)}, u32[]{:S(2)}) collective-permute-start(bf16[64,16,256]{2,1,0:T(8,128)(2,1)S(1)} %collective-permute-done.32.refs_12_), channel_id=1, source_target_pairs={{4,0},{6,2},{0,4},{2,6},{12,8},{14,10},{8,12},{10,14},{20,16},{22,... | collective-permute-start | bytes 1572872 | tf_op jit(solution)/shard_map/ppermute | solution.py:443
  325.7 94.1 %collective-permute-start.33 = (bf16[64,16,256]{2,1,0:T(8,128)(2,1)S(1)}, bf16[64,16,256]{2,1,0:T(8,128)(2,1)S(1)}, u32[]{:S(2)}, u32[]{:S(2)}) collective-permute-start(bf16[64,16,256]{2,1,0:T(8,128)(2,1)S(1)} %collective-permute-done.32.refs_12_), channel_id=1, source_target_pairs={{2,0},{0,2},{6,4},{4,6},{10,8},{8,10},{14,12},{12,14},{18,16},{16,... | collective-permute-start | bytes 1572872 | tf_op jit(solution)/shard_map/ppermute | solution.py:443
  328.5 91.2 %collective-permute-start.31 = (bf16[64,16,256]{2,1,0:T(8,128)(2,1)S(1)}, bf16[64,16,256]{2,1,0:T(8,128)(2,1)S(1)}, u32[]{:S(2)}, u32[]{:S(2)}) collective-permute-start(bf16[64,16,256]{2,1,0:T(8,128)(2,1)S(1)} %collective-permute-done.30.refs_10_), channel_id=1, source_target_pairs={{2,0},{0,2},{6,4},{4,6},{10,8},{8,10},{14,12},{12,14},{18,16},{16,... | collective-permute-start | bytes 1572872 | tf_op jit(solution)/shard_map/ppermute | solution.py:443
  328.6 91.2 %collective-permute-start.43 = (bf16[64,16,256]{2,1,0:T(8,128)(2,1)S(1)}, bf16[64,16,256]{2,1,0:T(8,128)(2,1)}, u32[]{:S(2)}, u32[]{:S(2)}) collective-permute-start(bf16[64,16,256]{2,1,0:T(8,128)(2,1)S(1)} %collective-permute-done.42.refs_22_), channel_id=1, source_target_pairs={{2,0},{0,2},{6,4},{4,6},{10,8},{8,10},{14,12},{12,14},{18,16},{16,... | collective-permute-start | bytes 1572872 | tf_op jit(solution)/shard_map/ppermute | solution.py:443
  329.1 90.7 %collective-permute-start.39 = (bf16[64,16,256]{2,1,0:T(8,128)(2,1)S(1)}, bf16[64,16,256]{2,1,0:T(8,128)(2,1)}, u32[]{:S(2)}, u32[]{:S(2)}) collective-permute-start(bf16[64,16,256]{2,1,0:T(8,128)(2,1)S(1)} %collective-permute-done.38.refs_18_), channel_id=1, source_target_pairs={{2,0},{0,2},{6,4},{4,6},{10,8},{8,10},{14,12},{12,14},{18,16},{16,... | collective-permute-start | bytes 1572872 | tf_op jit(solution)/shard_map/ppermute | solution.py:443
  336.3 84.4 %collective-permute-start.35 = (bf16[64,16,256]{2,1,0:T(8,128)(2,1)S(1)}, bf16[64,16,256]{2,1,0:T(8,128)(2,1)}, u32[]{:S(2)}, u32[]{:S(2)}) collective-permute-start(bf16[64,16,256]{2,1,0:T(8,128)(2,1)S(1)} %collective-permute-done.34.refs_14_), channel_id=1, source_target_pairs={{2,0},{0,2},{6,4},{4,6},{10,8},{8,10},{14,12},{12,14},{18,16},{16,... | collective-permute-start | bytes 1572872 | tf_op jit(solution)/shard_map/ppermute | solution.py:443
  (26 other events, 2156.8 us)
